TPU v7x, 256 devices: a whole 4x4x8 slice. The times are simulated.
256 devices in a mesh: paths: 256 (over x, y, z, core).
Axes of the slice: x: 4, y: 4, z: 8, core: 2. Of those that a mesh axis runs over, the one named last changes fastest.
Arguments:
- params: float32 [2048, 4], replicated, may hold values from -0.9 to 2, as said below
- increments: bfloat16 [2, 64, 32768], P(None, None, 'paths'), may hold values from -5 to 5
- w_in: bfloat16 [6, 1024], replicated, may hold values from -2.5 to 2.5
- b_in: float32 [1024], replicated, may hold values from -3 to 3
- w_mid: bfloat16 [1024, 1024], replicated, may hold values from -0.1875 to 0.1875
- b_mid: float32 [1024], replicated, may hold values from -3 to 3
- w_out: bfloat16 [1024], replicated, may hold values from -0.1875 to 0.1875
- b_out: float32 [1], replicated, may hold values from -3 to 3
Outputs:
- prices: float32 [2048, 88], P('paths')
- direction_w_in: float32 [6, 1024], replicated
- direction_b_in: float32 [1024], replicated
- direction_w_mid: float32 [1024, 1024], replicated
- direction_b_mid: float32 [1024], replicated
- direction_w_out: float32 [1024], replicated
- direction_b_out: float32 [1], replicated
Inputs may be any that keep to these rules, and one draw needn't show every extreme that they name: `params`: each row holds a Hurst index in [0.05, 0.45], a vol-of-vol in [0.8, 2.0], a correlation in [-0.9, -0.3] and an initial forward variance in [0.01, 0.15].
All inputs are finite; a program needn't handle non-finite values.
Results may differ from a plain program's by a relative error of at most 0.0003.
The roundings to bfloat16 on the way count: a program that leaves them out, or rounds other values in their place, can miss the bound.
Values sent between devices are 32-bit elements; how exact they have to be, the bound alone decides.
A program may use at most 64 MiB of HBM per device.

v0:
```python
import math

import jax
import jax.numpy as jnp
from jax import lax
from jax.sharding import PartitionSpec as P

STEPS = 64
MATS = 8
STRIKES = 11
PAIRS = 88


EPSILON = 1e-06


def strike_grid():
    tenors = (jnp.arange(MATS, dtype=jnp.float32) + 1.0) / MATS
    offsets = jnp.arange(STRIKES, dtype=jnp.float32) - (STRIKES - 1) / 2.0
    log_strike = 0.05 * offsets[None, :] * jnp.sqrt(tenors)[:, None]
    return (tenors, log_strike)


def payoff_sums(block_params, increments):
    count = block_params.shape[0]
    paths_here = increments.shape[2]
    hurst = block_params[:, 0]
    vol_of_vol = block_params[:, 1]
    correl = block_params[:, 2]
    forward_var = block_params[:, 3]
    delta_t = 1.0 / STEPS
    position = jnp.arange(STEPS, dtype=jnp.float32)
    lag = position[:, None] - position[None, :]
    lag_high = jnp.maximum(lag, 1.0)
    exponent = (hurst + 0.5)[:, None, None]
    powers = jnp.power(lag_high[None], exponent) - jnp.power(lag_high[None] - 1.0, exponent)
    front = jnp.sqrt(2.0 * hurst) * jnp.power(delta_t, hurst) / (hurst + 0.5)
    kernel = jnp.where((lag >= 1.0)[None], powers * front[:, None, None], 0.0).astype(jnp.bfloat16)
    drive = jnp.dot(
        kernel.reshape(count * STEPS, STEPS), increments[0], preferred_element_type=jnp.float32
    )
    drive = drive.reshape(count, STEPS, paths_here)
    times = position * delta_t
    compensator = (
        0.5
        * vol_of_vol[:, None]
        * vol_of_vol[:, None]
        * jnp.power(times[None, :], 2.0 * hurst[:, None])
    )
    variance = forward_var[:, None, None] * jnp.exp(
        vol_of_vol[:, None, None] * drive - compensator[:, :, None]
    )
    first_noise = increments[0].astype(jnp.float32)
    second_noise = increments[1].astype(jnp.float32)
    shock = (
        correl[:, None, None] * first_noise[None]
        + jnp.sqrt(1.0 - correl * correl)[:, None, None] * second_noise[None]
    )
    moves = jnp.sqrt(variance * delta_t) * shock - 0.5 * delta_t * variance
    log_spot = jnp.cumsum(moves.reshape(count, MATS, STEPS // MATS, paths_here).sum(axis=2), axis=1)
    tenors, log_strike = strike_grid()
    spot = jnp.exp(log_spot)
    gains = jnp.maximum(spot[:, :, None, :] - jnp.exp(log_strike)[None, :, :, None], 0.0)
    return jnp.sum(gains, axis=3).reshape(count, PAIRS)


def evolve(set_rows, increments, total_paths):
    count = set_rows.shape[0]
    block = math.gcd(count, 128)
    groups = set_rows.reshape(count // block, block, 4)
    sums = lax.map(lambda group: payoff_sums(group, increments), groups)
    return sums.reshape(count, PAIRS) / total_paths


def features(set_rows):
    count = set_rows.shape[0]
    tenors, log_strike = strike_grid()
    scaled = set_rows * jnp.array([4.0, 1.0, 1.0, 20.0], dtype=jnp.float32)
    per_pair = jnp.stack([4.0 * log_strike.reshape(PAIRS), jnp.repeat(tenors, STRIKES)], axis=1)
    left = jnp.broadcast_to(scaled[:, None, :], (count, PAIRS, 4))
    right = jnp.broadcast_to(per_pair[None], (count, PAIRS, 2))
    return jnp.concatenate([left, right], axis=2).reshape(count * PAIRS, 6).astype(jnp.bfloat16)


def silu_slope(value):
    logistic = jax.nn.sigmoid(value)
    return logistic * (1.0 + value * (1.0 - logistic))


def contract_rows(left, right):
    return lax.dot_general(
        left, right, (((0,), (0,)), ((), ())), preferred_element_type=jnp.float32
    )


def local_terms(inputs, target, w_in, b_in, w_mid, b_mid, w_out, b_out, inv_sets):
    raw_in = jnp.dot(inputs, w_in, preferred_element_type=jnp.float32) + b_in
    hidden_in = jax.nn.silu(raw_in).astype(jnp.bfloat16)
    raw_mid = jnp.dot(hidden_in, w_mid, preferred_element_type=jnp.float32) + b_mid
    hidden_mid = jax.nn.silu(raw_mid).astype(jnp.bfloat16)
    predicted = jnp.dot(hidden_mid, w_out, preferred_element_type=jnp.float32) + b_out[0]
    slope = (predicted - target) * inv_sets
    grad_out = jnp.sum(hidden_mid.astype(jnp.float32) * slope[:, None], axis=0)
    grad_bout = jnp.sum(slope, keepdims=True)
    delta_mid = (slope[:, None] * w_out.astype(jnp.float32)[None, :] * silu_slope(raw_mid)).astype(
        jnp.bfloat16
    )
    grad_bmid = jnp.sum(delta_mid.astype(jnp.float32), axis=0)
    backward = lax.dot_general(
        delta_mid, w_mid, (((1,), (1,)), ((), ())), preferred_element_type=jnp.float32
    )
    delta_in = (backward * silu_slope(raw_in)).astype(jnp.bfloat16)
    grad_in = contract_rows(inputs, delta_in)
    grad_bin = jnp.sum(delta_in.astype(jnp.float32), axis=0)
    return ((grad_in, grad_bin, grad_bmid, grad_out, grad_bout), hidden_in, delta_mid)


def directions(grad_w, grad_b):
    entries = grad_w.size + grad_b.size
    mean_square = (jnp.sum(grad_w * grad_w) + jnp.sum(grad_b * grad_b)) / entries
    factor = lax.rsqrt(mean_square + EPSILON)
    return (grad_w * factor, grad_b * factor)


def on_device(params, increments, w_in, b_in, w_mid, b_mid, w_out, b_out):
    devices = lax.axis_size("paths")
    total_paths = increments.shape[2] * devices
    set_count = params.shape[0]
    set_dev = set_count // devices
    owner = lax.axis_index("paths")
    every_set = evolve(params, increments, total_paths)
    summed = lax.psum(every_set, "paths")
    prices = lax.dynamic_slice_in_dim(summed, owner * set_dev, set_dev, 0)
    own_params = lax.dynamic_slice_in_dim(params, owner * set_dev, set_dev, 0)
    small, hidden_in, delta_mid = local_terms(
        features(own_params),
        prices.reshape(-1),
        w_in,
        b_in,
        w_mid,
        b_mid,
        w_out,
        b_out,
        1.0 / set_count,
    )
    grad_mid = contract_rows(hidden_in, delta_mid)
    grad_in, grad_bin, grad_bmid, grad_out, grad_bout, grad_mid = lax.psum(
        (small[0], small[1], small[2], small[3], small[4], grad_mid), "paths"
    )
    direction_w_mid, direction_b_mid = directions(grad_mid, grad_bmid)
    direction_w_in, direction_b_in = directions(grad_in, grad_bin)
    direction_w_out, direction_b_out = directions(grad_out, grad_bout)
    return (
        prices,
        direction_w_in,
        direction_b_in,
        direction_w_mid,
        direction_b_mid,
        direction_w_out,
        direction_b_out,
    )


def solution(mesh):
    in_specs = (P(), P(None, None, "paths"), P(), P(), P(), P(), P(), P())
    out_specs = (P("paths", None), P(), P(), P(), P(), P(), P())
    return jax.shard_map(
        on_device, mesh=mesh, in_specs=in_specs, out_specs=out_specs, check_vma=False
    )
```

profile of v0, /device:TPU:1, one launch (start us, length us, event | category | flops | bytes accessed | tf_op | source)
XLA Modules:
  0.0 800.8 jit_solution(9235919983980446426)
XLA Ops:
  7.2 233.0 %while.12 = (s32[]{:T(128)}, f32[16,128,88]{1,2,0:T(8,128)}, f32[16,128,4]{1,2,0:T(4,128)}, bf16[2,64,128]{2,1,0:T(8,128)(2,1)}, s32[]{:T(128)}) while((s32[]{:T(128)}, f32[16,128,88]{1,2,0:T(8,128)}, f32[16,128,4]{1,2,0:T(4,128)}, bf16[2,64,128]{2,1,0:T(8,128)(2,1)}, s32[]{:T(128)}) %tuple.59), condition=%wide.region_4.5_spmd, body=%wide.region_0.4_spmd.sunk | while | flops 152996288 | bytes 3797413 | solution.py:71
  9.1 9.3 %bitcast_reduce_fusion.2 = f32[128,8,128]{2,0,1:T(8,128)S(1)} fusion(f32[64,128]{1,0:T(8,128)S(1)} %get-tuple-element.135, f32[128]{0:T(128)S(1)} %get-tuple-element.136, f32[64,128]{1,0:T(8,128)S(1)} %get-tuple-element.137, f32[128]{0:T(128)S(1)} %get-tuple-element.138, f32[128,64]{0,1:T(8,128)S(1)} %power_multiply_fusion.2, ...), kind=kOutput, calls=%fused_computation.1.clone.1 | convolution fusion | flops 147718144 | bytes 678912 | tf_op jit(solution)/shard_map/while/body/eval_jaxpr/dot_general | solution.py:39
  23.7 9.3 %bitcast_reduce_fusion.2 = f32[128,8,128]{2,0,1:T(8,128)S(1)} fusion(f32[64,128]{1,0:T(8,128)S(1)} %get-tuple-element.135, f32[128]{0:T(128)S(1)} %get-tuple-element.136, f32[64,128]{1,0:T(8,128)S(1)} %get-tuple-element.137, f32[128]{0:T(128)S(1)} %get-tuple-element.138, f32[128,64]{0,1:T(8,128)S(1)} %power_multiply_fusion.2, ...), kind=kOutput, calls=%fused_computation.1.clone.1 | convolution fusion | flops 147718144 | bytes 678912 | tf_op jit(solution)/shard_map/while/body/eval_jaxpr/dot_general | solution.py:39
  38.2 9.3 %bitcast_reduce_fusion.2 = f32[128,8,128]{2,0,1:T(8,128)S(1)} fusion(f32[64,128]{1,0:T(8,128)S(1)} %get-tuple-element.135, f32[128]{0:T(128)S(1)} %get-tuple-element.136, f32[64,128]{1,0:T(8,128)S(1)} %get-tuple-element.137, f32[128]{0:T(128)S(1)} %get-tuple-element.138, f32[128,64]{0,1:T(8,128)S(1)} %power_multiply_fusion.2, ...), kind=kOutput, calls=%fused_computation.1.clone.1 | convolution fusion | flops 147718144 | bytes 678912 | tf_op jit(solution)/shard_map/while/body/eval_jaxpr/dot_general | solution.py:39
  52.8 9.3 %bitcast_reduce_fusion.2 = f32[128,8,128]{2,0,1:T(8,128)S(1)} fusion(f32[64,128]{1,0:T(8,128)S(1)} %get-tuple-element.135, f32[128]{0:T(128)S(1)} %get-tuple-element.136, f32[64,128]{1,0:T(8,128)S(1)} %get-tuple-element.137, f32[128]{0:T(128)S(1)} %get-tuple-element.138, f32[128,64]{0,1:T(8,128)S(1)} %power_multiply_fusion.2, ...), kind=kOutput, calls=%fused_computation.1.clone.1 | convolution fusion | flops 147718144 | bytes 678912 | tf_op jit(solution)/shard_map/while/body/eval_jaxpr/dot_general | solution.py:39
  67.3 9.3 %bitcast_reduce_fusion.2 = f32[128,8,128]{2,0,1:T(8,128)S(1)} fusion(f32[64,128]{1,0:T(8,128)S(1)} %get-tuple-element.135, f32[128]{0:T(128)S(1)} %get-tuple-element.136, f32[64,128]{1,0:T(8,128)S(1)} %get-tuple-element.137, f32[128]{0:T(128)S(1)} %get-tuple-element.138, f32[128,64]{0,1:T(8,128)S(1)} %power_multiply_fusion.2, ...), kind=kOutput, calls=%fused_computation.1.clone.1 | convolution fusion | flops 147718144 | bytes 678912 | tf_op jit(solution)/shard_map/while/body/eval_jaxpr/dot_general | solution.py:39
  81.9 9.3 %bitcast_reduce_fusion.2 = f32[128,8,128]{2,0,1:T(8,128)S(1)} fusion(f32[64,128]{1,0:T(8,128)S(1)} %get-tuple-element.135, f32[128]{0:T(128)S(1)} %get-tuple-element.136, f32[64,128]{1,0:T(8,128)S(1)} %get-tuple-element.137, f32[128]{0:T(128)S(1)} %get-tuple-element.138, f32[128,64]{0,1:T(8,128)S(1)} %power_multiply_fusion.2, ...), kind=kOutput, calls=%fused_computation.1.clone.1 | convolution fusion | flops 147718144 | bytes 678912 | tf_op jit(solution)/shard_map/while/body/eval_jaxpr/dot_general | solution.py:39
  96.4 9.3 %bitcast_reduce_fusion.2 = f32[128,8,128]{2,0,1:T(8,128)S(1)} fusion(f32[64,128]{1,0:T(8,128)S(1)} %get-tuple-element.135, f32[128]{0:T(128)S(1)} %get-tuple-element.136, f32[64,128]{1,0:T(8,128)S(1)} %get-tuple-element.137, f32[128]{0:T(128)S(1)} %get-tuple-element.138, f32[128,64]{0,1:T(8,128)S(1)} %power_multiply_fusion.2, ...), kind=kOutput, calls=%fused_computation.1.clone.1 | convolution fusion | flops 147718144 | bytes 678912 | tf_op jit(solution)/shard_map/while/body/eval_jaxpr/dot_general | solution.py:39
  111.0 9.3 %bitcast_reduce_fusion.2 = f32[128,8,128]{2,0,1:T(8,128)S(1)} fusion(f32[64,128]{1,0:T(8,128)S(1)} %get-tuple-element.135, f32[128]{0:T(128)S(1)} %get-tuple-element.136, f32[64,128]{1,0:T(8,128)S(1)} %get-tuple-element.137, f32[128]{0:T(128)S(1)} %get-tuple-element.138, f32[128,64]{0,1:T(8,128)S(1)} %power_multiply_fusion.2, ...), kind=kOutput, calls=%fused_computation.1.clone.1 | convolution fusion | flops 147718144 | bytes 678912 | tf_op jit(solution)/shard_map/while/body/eval_jaxpr/dot_general | solution.py:39
  125.5 9.3 %bitcast_reduce_fusion.2 = f32[128,8,128]{2,0,1:T(8,128)S(1)} fusion(f32[64,128]{1,0:T(8,128)S(1)} %get-tuple-element.135, f32[128]{0:T(128)S(1)} %get-tuple-element.136, f32[64,128]{1,0:T(8,128)S(1)} %get-tuple-element.137, f32[128]{0:T(128)S(1)} %get-tuple-element.138, f32[128,64]{0,1:T(8,128)S(1)} %power_multiply_fusion.2, ...), kind=kOutput, calls=%fused_computation.1.clone.1 | convolution fusion | flops 147718144 | bytes 678912 | tf_op jit(solution)/shard_map/while/body/eval_jaxpr/dot_general | solution.py:39
  140.1 9.3 %bitcast_reduce_fusion.2 = f32[128,8,128]{2,0,1:T(8,128)S(1)} fusion(f32[64,128]{1,0:T(8,128)S(1)} %get-tuple-element.135, f32[128]{0:T(128)S(1)} %get-tuple-element.136, f32[64,128]{1,0:T(8,128)S(1)} %get-tuple-element.137, f32[128]{0:T(128)S(1)} %get-tuple-element.138, f32[128,64]{0,1:T(8,128)S(1)} %power_multiply_fusion.2, ...), kind=kOutput, calls=%fused_computation.1.clone.1 | convolution fusion | flops 147718144 | bytes 678912 | tf_op jit(solution)/shard_map/while/body/eval_jaxpr/dot_general | solution.py:39
  154.7 9.3 %bitcast_reduce_fusion.2 = f32[128,8,128]{2,0,1:T(8,128)S(1)} fusion(f32[64,128]{1,0:T(8,128)S(1)} %get-tuple-element.135, f32[128]{0:T(128)S(1)} %get-tuple-element.136, f32[64,128]{1,0:T(8,128)S(1)} %get-tuple-element.137, f32[128]{0:T(128)S(1)} %get-tuple-element.138, f32[128,64]{0,1:T(8,128)S(1)} %power_multiply_fusion.2, ...), kind=kOutput, calls=%fused_computation.1.clone.1 | convolution fusion | flops 147718144 | bytes 678912 | tf_op jit(solution)/shard_map/while/body/eval_jaxpr/dot_general | solution.py:39
  169.2 9.3 %bitcast_reduce_fusion.2 = f32[128,8,128]{2,0,1:T(8,128)S(1)} fusion(f32[64,128]{1,0:T(8,128)S(1)} %get-tuple-element.135, f32[128]{0:T(128)S(1)} %get-tuple-element.136, f32[64,128]{1,0:T(8,128)S(1)} %get-tuple-element.137, f32[128]{0:T(128)S(1)} %get-tuple-element.138, f32[128,64]{0,1:T(8,128)S(1)} %power_multiply_fusion.2, ...), kind=kOutput, calls=%fused_computation.1.clone.1 | convolution fusion | flops 147718144 | bytes 678912 | tf_op jit(solution)/shard_map/while/body/eval_jaxpr/dot_general | solution.py:39
  183.8 9.3 %bitcast_reduce_fusion.2 = f32[128,8,128]{2,0,1:T(8,128)S(1)} fusion(f32[64,128]{1,0:T(8,128)S(1)} %get-tuple-element.135, f32[128]{0:T(128)S(1)} %get-tuple-element.136, f32[64,128]{1,0:T(8,128)S(1)} %get-tuple-element.137, f32[128]{0:T(128)S(1)} %get-tuple-element.138, f32[128,64]{0,1:T(8,128)S(1)} %power_multiply_fusion.2, ...), kind=kOutput, calls=%fused_computation.1.clone.1 | convolution fusion | flops 147718144 | bytes 678912 | tf_op jit(solution)/shard_map/while/body/eval_jaxpr/dot_general | solution.py:39
  198.3 9.3 %bitcast_reduce_fusion.2 = f32[128,8,128]{2,0,1:T(8,128)S(1)} fusion(f32[64,128]{1,0:T(8,128)S(1)} %get-tuple-element.135, f32[128]{0:T(128)S(1)} %get-tuple-element.136, f32[64,128]{1,0:T(8,128)S(1)} %get-tuple-element.137, f32[128]{0:T(128)S(1)} %get-tuple-element.138, f32[128,64]{0,1:T(8,128)S(1)} %power_multiply_fusion.2, ...), kind=kOutput, calls=%fused_computation.1.clone.1 | convolution fusion | flops 147718144 | bytes 678912 | tf_op jit(solution)/shard_map/while/body/eval_jaxpr/dot_general | solution.py:39
  212.9 9.3 %bitcast_reduce_fusion.2 = f32[128,8,128]{2,0,1:T(8,128)S(1)} fusion(f32[64,128]{1,0:T(8,128)S(1)} %get-tuple-element.135, f32[128]{0:T(128)S(1)} %get-tuple-element.136, f32[64,128]{1,0:T(8,128)S(1)} %get-tuple-element.137, f32[128]{0:T(128)S(1)} %get-tuple-element.138, f32[128,64]{0,1:T(8,128)S(1)} %power_multiply_fusion.2, ...), kind=kOutput, calls=%fused_computation.1.clone.1 | convolution fusion | flops 147718144 | bytes 678912 | tf_op jit(solution)/shard_map/while/body/eval_jaxpr/dot_general | solution.py:39
  227.4 9.3 %bitcast_reduce_fusion.2 = f32[128,8,128]{2,0,1:T(8,128)S(1)} fusion(f32[64,128]{1,0:T(8,128)S(1)} %get-tuple-element.135, f32[128]{0:T(128)S(1)} %get-tuple-element.136, f32[64,128]{1,0:T(8,128)S(1)} %get-tuple-element.137, f32[128]{0:T(128)S(1)} %get-tuple-element.138, f32[128,64]{0,1:T(8,128)S(1)} %power_multiply_fusion.2, ...), kind=kOutput, calls=%fused_computation.1.clone.1 | convolution fusion | flops 147718144 | bytes 678912 | tf_op jit(solution)/shard_map/while/body/eval_jaxpr/dot_general | solution.py:39
  245.1 4.3 multiply_convert_fusion.2
  251.1 250.1 %all-reduce.4.cloned.1.call-done = f32[2048,88]{1,0:T(8,128)} async-done(((f32[2048,88]{1,0:T(8,128)}), f32[2048,88]{1,0:T(8,128)}) %all-reduce.4.cloned.1.call-update) | async-done | bytes 720912 | tf_op jit(solution)/shard_map/psum | solution.py:132
  505.2 4.1 convert_reduce_fusion
  515.7 4.7 convert_reduce_fusion.1
  520.7 79.2 %all-reduce = (f32[6,1024]{1,0:T(8,128)S(1)}, f32[1024]{0:T(1024)S(1)}, f32[1024]{0:T(1024)S(1)}, f32[1024]{0:T(1024)S(1)}, f32[1]{0:T(128)}) all-reduce(f32[6,1024]{1,0:T(8,128)S(1)} %fusion.17, f32[1024]{0:T(1024)} %get-tuple-element.94, f32[1024]{0:T(1024)S(1)} %get-tuple-element.77, ...), channel_id=1, replica_groups=mesh['paths'=256] {'paths'}, use_global_device_ids=true, to_apply=%region_6.7 | all-reduce | flops 9217 | bytes 73736 | tf_op jit(solution)/shard_map/psum | solution.py:147
  607.5 174.5 %all-reduce.6.cloned.1.call-done = f32[1024,1024]{1,0:T(8,128)} async-done(((f32[1024,1024]{1,0:T(8,128)}), f32[1024,1024]{1,0:T(8,128)}) %all-reduce.6.cloned.1.call-update) | async-done | bytes 4194320 | tf_op jit(solution)/shard_map/psum | solution.py:147
  787.8 5.0 broadcast_multiply_fusion
  (329 shorter events, 108.2 us)
Async XLA Ops:
  7.2 237.9 %copy-start = (bf16[1024,1024]{1,0:T(8,128)(2,1)S(1)}, bf16[1024,1024]{1,0:T(8,128)(2,1)}, u32[]{:S(2)}) copy-start(bf16[1024,1024]{1,0:T(8,128)(2,1)} %param.15) | copy-start | bytes 6291460
  7.2 494.1 %all-reduce.4.cloned.1.call-start = ((), (), s32[]{:S(2)}) async-start(), calls=%async_computation | async-start | bytes 2097152 | tf_op jit(solution)/shard_map/psum | solution.py:132
  240.2 3.2 copy-start.8
  240.2 4.2 copy-start.5
  241.4 3.6 copy-start.7
  242.8 539.2 %all-reduce.6.cloned.1.call-start = ((), (), s32[]{:S(2)}) async-start(), calls=%async_computation.1 | async-start | bytes 8388608 | tf_op jit(solution)/shard_map/psum | solution.py:147
  245.0 4.3 copy-start.1
  245.0 4.3 copy-start.6
  505.2 5.2 copy-start.2
  505.2 5.2 copy-start.9
  509.3 1.1 copy-start.3
  514.3 1.4 copy-start.4
Sparse Core Ops, SparseCore 0:
  243.0 258.2 all-reduce.3
  514.5 267.4 all-reduce.5
where the time goes:
time: 807 us; the launch traced here: 801 us
  waiting for transfers between devices  425 us (53%)
  matrix products  163 us (20%)
  blocking collectives  79.2 us (10%)
  other arithmetic  72 us (9%)
  local copies, waits for them, and re-layouts  39.8 us (5%)
  between operations  21.2 us (3%)
    psum x1, waiting for transfers between devices, on_device(): summed = lax.psum(every_set, 'paths')  250 us
    psum x1, waiting for transfers between devices, on_device(): lax.psum((small[0], small[1], small[2], small[3], small[4], grad_mid), 'p...  175 us
    dot_general x16, matrix products, payoff_sums(): jnp.dot(kernel.reshape(count * STEPS, STEPS), increments[0], preferred_el...  148 us
    psum x1, blocking collectives, on_device(): lax.psum((small[0], small[1], small[2], small[3], small[4], grad_mid), 'p...  79.2 us
    reduce_sum x16, other arithmetic, payoff_sums(): return jnp.sum(gains, axis=3).reshape(count, PAIRS)  26.2 us
  transfers between devices with their start and end apart: 2, of which 2 were waited for; matrix products, arithmetic and copies ran while one was open for 2% of the time, Pallas kernels for 0%

commit v1 on v0

v1 whole, which is shorter than its diff:
```python
import math

import jax
import jax.numpy as jnp
from jax import lax
from jax.experimental import pallas as pl
from jax.experimental.pallas import tpu as pltpu
from jax.sharding import PartitionSpec as P

STEPS = 64
MATS = 8
STRIKES = 11
PAIRS = 88
EPSILON = 1e-06
LOG2E = 1.4426950408889634
NX, NY, NZ, NC = 4, 4, 8, 2
OWN = 8
BLOCK = NY * NZ * OWN
BLOCKS = NX * NC
MESH = pl.DeviceIdType.MESH


def strike_grid():
    tenors = (jnp.arange(MATS, dtype=jnp.float32) + 1.0) / MATS
    offsets = jnp.arange(STRIKES, dtype=jnp.float32) - (STRIKES - 1) / 2.0
    log_strike = 0.05 * offsets[None, :] * jnp.sqrt(tenors)[:, None]
    return (tenors, log_strike)


def strike_values():
    return [
        [math.exp(0.05 * (j - 5) * math.sqrt((m + 1) / MATS)) for j in range(STRIKES)]
        for m in range(MATS)
    ]


def round_bf16(x):
    return lax.reduce_precision(x, 8, 7)


def coords(index):
    core = index % NC
    z = (index // NC) % NZ
    y = (index // (NC * NZ)) % NY
    x = index // (NC * NZ * NY)
    return x, y, z, core


def device_at(x, y, z, core):
    return ((x * NY + y) * NZ + z) * NC + core


def set_operands(params):
    hurst, vol, correl, forward = (params[:, k : k + 1] for k in range(4))
    delta_t = 1.0 / STEPS
    lag = jnp.arange(STEPS, dtype=jnp.float32)[None, :]
    high = jnp.maximum(lag, 1.0)
    expo = hurst + 0.5
    powers = jnp.power(high, expo) - jnp.power(high - 1.0, expo)
    front = jnp.sqrt(2.0 * hurst) * jnp.power(delta_t, hurst) / (hurst + 0.5)
    kern = round_bf16(jnp.where(lag >= 1.0, powers * front, 0.0))
    half = (0.5 * LOG2E) * vol
    weight = kern * half
    times = lag * delta_t
    comp = -0.5 * vol * half * jnp.power(times, 2.0 * hurst)
    mix = jnp.sqrt(1.0 - correl * correl)
    const = 0.5 * jnp.log2(forward * delta_t) - 1.0 - jnp.log2(mix)
    w_hi = round_bf16(weight)
    w_lo = round_bf16(weight - w_hi)
    c_hi = round_bf16(comp)
    c_lo = round_bf16(comp - c_hi)
    k_hi = round_bf16(const)
    k_lo = round_bf16(const - k_hi)
    k_ll = const - k_hi - k_lo
    first = lag < 0.5
    rows = jnp.concatenate(
        [
            jnp.where(first, k_hi, w_hi),
            jnp.where(first, k_lo, w_lo),
            jnp.where(first, k_ll, c_hi),
            jnp.where(first, 0.0, c_lo),
        ],
        axis=1,
    ).astype(jnp.bfloat16)
    ratio = jnp.broadcast_to(correl / mix, (params.shape[0], 128))
    scale = (2.0 * LOG2E) * (mix * mix)
    return rows, ratio, scale.reshape(1, -1)


def price_peers(x, y, z, core):
    mine = x * NC + core
    blocks = []
    for b in range(BLOCKS - 1):
        other = (mine + 1 + b) % BLOCKS
        blocks.append(device_at(other // NC, y, z, other % NC))
    along_y = [device_at(x, (y + d) % NY, z, core) for d in range(1, NY)]
    along_z = [device_at(x, y, (z + d) % NZ, core) for d in range(1, NZ)]
    return blocks, along_y, along_z


def prices_kernel(
    rows_ref,
    ratio_ref,
    scale_ref,
    inc_ref,
    out_ref,
    noise,
    table,
    walk,
    part,
    sent,
    got,
    got_y,
    got_z,
    send_sem,
    got_sem,
    send_y,
    got_y_sem,
    send_z,
    got_z_sem,
):
    step = pl.program_id(0)
    x, y, z, core = coords(lax.axis_index("paths"))
    blocks, along_y, along_z = price_peers(x, y, z, core)

    @pl.when(step == 0)
    def _():
        barrier = pltpu.get_barrier_semaphore()
        for peer in blocks + along_y + along_z:
            pl.semaphore_signal(barrier, inc=1, device_id=(peer,), device_id_type=MESH)
        noise[0] = inc_ref[0].astype(jnp.float32)
        noise[1] = inc_ref[1].astype(jnp.float32)
        part[...] = jnp.zeros_like(part)
        row = lax.broadcasted_iota(jnp.int32, (STEPS, 128), 0)
        for j in range(STEPS):
            walk[pl.ds(STEPS - 1 - j, 1), :] = noise[0, pl.ds(j, 1), :]
        walk[pl.ds(STEPS, STEPS), :] = jnp.zeros((STEPS, 128), jnp.float32)
        one = jnp.ones((STEPS, 128), jnp.float32)
        for i in range(STEPS):
            past = walk[pl.ds(STEPS - 1 - i, STEPS), :]
            past = jnp.where(row == 0, one, past).astype(jnp.bfloat16)
            pick = jnp.where(row == i, 1.0, 0.0)
            hot = jnp.where(row == 0, one, pick).astype(jnp.bfloat16)
            hot_lo = jnp.where(row == 0, 0.0, pick).astype(jnp.bfloat16)
            cols = pl.ds((i % 2) * 128, 128)
            table[i // 2, pl.ds(0, STEPS), cols] = past
            table[i // 2, pl.ds(STEPS, STEPS), cols] = past
            table[i // 2, pl.ds(2 * STEPS, STEPS), cols] = hot
            table[i // 2, pl.ds(3 * STEPS, STEPS), cols] = hot_lo

    strikes = strike_values()
    walk[...] = jnp.zeros_like(walk)
    scale = scale_ref[...]
    for m in range(MATS):
        for q in range(4):
            pair = jnp.dot(
                rows_ref[...], table[m * 4 + q], preferred_element_type=jnp.float32
            )
            for h in range(2):
                i = m * 8 + q * 2 + h
                vol = jnp.exp2(pair[:, h * 128 : (h + 1) * 128])
                shock = ratio_ref[...] * noise[0, pl.ds(i, 1), :] + noise[1, pl.ds(i, 1), :]
                walk[...] += vol * (shock - vol)
        spot = jnp.exp2(walk[...].T * scale)
        for j in range(STRIKES):
            k = strikes[m][j]
            top = jnp.sum(jnp.maximum(spot, k).reshape(16, 8, BLOCK), axis=0)
            part[pl.ds(m * STRIKES + j, 1), :] = jnp.sum(top - 16.0 * k, axis=0, keepdims=True)
    sent[step] = part[...].T

    @pl.when(step == 0)
    def _():
        pl.semaphore_wait(pltpu.get_barrier_semaphore(), len(blocks + along_y + along_z))

    def block_copy(b):
        other = (x * NC + core + 1 + b) % BLOCKS
        return pltpu.make_async_remote_copy(
            src_ref=sent.at[b],
            dst_ref=got.at[b],
            send_sem=send_sem.at[b],
            recv_sem=got_sem.at[b],
            device_id=(device_at(other // NC, y, z, other % NC),),
            device_id_type=MESH,
        )

    @pl.when(step < BLOCKS - 1)
    def _():
        block_copy(step).start()

    @pl.when(step == BLOCKS - 1)
    def _():
        total = sent.at[BLOCKS - 1]
        for b in range(BLOCKS - 1):
            block_copy(b).wait_recv()
            total[...] += got[b]
        rows_y = NZ * OWN

        def y_rows(d):
            return pl.ds(pl.multiple_of(((y + d) % NY) * rows_y, rows_y), rows_y)

        copies = []
        for d in range(1, NY):
            copy = pltpu.make_async_remote_copy(
                src_ref=total.at[y_rows(d), :],
                dst_ref=got_y.at[d],
                send_sem=send_y.at[d],
                recv_sem=got_y_sem.at[d],
                device_id=(along_y[d - 1],),
                device_id_type=MESH,
            )
            copy.start()
            copies.append(copy)
        own = total[y_rows(0), :]
        for d in range(1, NY):
            copies[d - 1].wait_recv()
            own = own + got_y[d]
        got_y[0] = own

        def z_rows(d):
            return pl.ds(pl.multiple_of(((z + d) % NZ) * OWN, OWN), OWN)

        for d in range(1, NZ):
            copy = pltpu.make_async_remote_copy(
                src_ref=got_y.at[0, z_rows(d), :],
                dst_ref=got_z.at[d],
                send_sem=send_z.at[d],
                recv_sem=got_z_sem.at[d],
                device_id=(along_z[d - 1],),
                device_id_type=MESH,
            )
            copy.start()
            copies.append(copy)
        final = got_y[0, z_rows(0), :]
        for d in range(1, NZ):
            copies[NY - 1 + d - 1].wait_recv()
            final = final + got_z[d]
        out_ref[...] = final
        for b in range(BLOCKS - 1):
            block_copy(b).wait_send()
        for copy in copies:
            copy.wait_send()


def price_sums(params, increments):
    index = lax.axis_index("paths")
    x, y, z, core = coords(index)
    order = params.reshape(NX, NY, NZ, NC, OWN, 4).transpose(0, 3, 1, 2, 4, 5)
    order = order.reshape(BLOCKS, BLOCK, 4)
    order = jnp.concatenate([order, order], axis=0)
    order = lax.dynamic_slice_in_dim(order, x * NC + core + 1, BLOCKS, 0)
    rows, ratio, scale = set_operands(order.reshape(BLOCKS * BLOCK, 4))
    return pl.pallas_call(
        prices_kernel,
        grid=(BLOCKS,),
        in_specs=[
            pl.BlockSpec((BLOCK, 256), lambda b: (b, 0)),
            pl.BlockSpec((BLOCK, 128), lambda b: (b, 0)),
            pl.BlockSpec((1, BLOCK), lambda b: (0, b)),
            pl.BlockSpec((2, STEPS, 128), lambda b: (0, 0, 0)),
        ],
        out_specs=pl.BlockSpec((OWN, 128), lambda b: (0, 0)),
        out_shape=jax.ShapeDtypeStruct((OWN, 128), jnp.float32),
        scratch_shapes=[
            pltpu.VMEM((2, STEPS, 128), jnp.float32),
            pltpu.VMEM((STEPS // 2, 256, 256), jnp.bfloat16),
            pltpu.VMEM((BLOCK, 128), jnp.float32),
            pltpu.VMEM((128, BLOCK), jnp.float32),
            pltpu.VMEM((BLOCKS, BLOCK, 128), jnp.float32),
            pltpu.VMEM((BLOCKS - 1, BLOCK, 128), jnp.float32),
            pltpu.VMEM((NY, NZ * OWN, 128), jnp.float32),
            pltpu.VMEM((NZ, OWN, 128), jnp.float32),
            pltpu.SemaphoreType.DMA((BLOCKS,)),
            pltpu.SemaphoreType.DMA((BLOCKS,)),
            pltpu.SemaphoreType.DMA((NY,)),
            pltpu.SemaphoreType.DMA((NY,)),
            pltpu.SemaphoreType.DMA((NZ,)),
            pltpu.SemaphoreType.DMA((NZ,)),
        ],
        compiler_params=pltpu.CompilerParams(collective_id=0, has_side_effects=True),
        name="prices",
    )(rows, ratio, scale, increments)


WIDE = 1024
HALF = WIDE // NC
ROWS_A = WIDE // NX
ROWS_B = ROWS_A // NY
ROWS_Z = ROWS_B // NZ
SMALL = 16
SLICE = HALF // NX


def sum_kernel(
    big_ref,
    small_ref,
    big_out,
    small_out,
    got_c,
    half,
    got_a,
    mid,
    got_b,
    low,
    got_z,
    s_got_c,
    s_got_a,
    s_b,
    s_z,
    s_sum,
    send_sem,
    recv_sem,
):
    x, y, z, core = coords(lax.axis_index("paths"))
    a = x * (1 - core) + y * core
    b = y * (1 - core) + x * core

    def at(aa, bb, zz):
        return device_at(aa * (1 - core) + bb * core, bb * (1 - core) + aa * core, zz, core)

    partner = device_at(x, y, z, 1 - core)
    along_a = [at((a + d) % NX, b, z) for d in range(1, NX)]
    along_b = [at(a, (b + d) % NY, z) for d in range(1, NY)]
    along_z = [at(a, b, (z + d) % NZ) for d in range(1, NZ)]
    peers = [partner] + along_a + along_b + along_z
    barrier = pltpu.get_barrier_semaphore()
    for peer in peers:
        pl.semaphore_signal(barrier, inc=1, device_id=(peer,), device_id_type=MESH)
    pl.semaphore_wait(barrier, len(peers))

    count = [0]
    started = []

    def send(src, dst, peer):
        k = count[0]
        count[0] += 1
        copy = pltpu.make_async_remote_copy(
            src_ref=src,
            dst_ref=dst,
            send_sem=send_sem.at[k],
            recv_sem=recv_sem.at[k],
            device_id=(peer,),
            device_id_type=MESH,
        )
        copy.start()
        started.append(copy)
        return copy

    def part(index, size):
        return pl.ds(pl.multiple_of(index * size, size), size)

    own_cols, other_cols = part(core, HALF), part(1 - core, HALF)
    big = send(big_ref.at[:, other_cols], got_c, partner)
    little = send(small_ref.at[:, other_cols], s_got_c, partner)
    little.wait_recv()
    s_got_c[...] += small_ref[:, own_cols]
    big.wait_recv()
    half[...] = big_ref[:, own_cols] + got_c[...]

    bigs, littles = [], []
    for d in range(1, NX):
        aa = (a + d) % NX
        bigs.append(send(half.at[part(aa, ROWS_A), :], got_a.at[d - 1], along_a[d - 1]))
        littles.append(send(s_got_c.at[:, part(aa, SLICE)], s_got_a.at[d - 1], along_a[d - 1]))
    for d in range(1, NX):
        littles[d - 1].wait_recv()
    s_b[b] = s_got_c[:, part(a, SLICE)] + s_got_a[0] + s_got_a[1] + s_got_a[2]
    for d in range(1, NX):
        bigs[d - 1].wait_recv()
    mid[...] = half[part(a, ROWS_A), :] + got_a[0] + got_a[1] + got_a[2]

    bigs, littles = [], []
    for d in range(1, NY):
        bb = (b + d) % NY
        bigs.append(send(mid.at[part(bb, ROWS_B), :], got_b.at[d - 1], along_b[d - 1]))
        littles.append(send(s_b.at[b], s_b.at[b], along_b[d - 1]))
    for d in range(1, NY):
        littles[d - 1].wait_recv()
    s_z[z] = (s_b[0] + s_b[1]) + (s_b[2] + s_b[3])
    for d in range(1, NY):
        bigs[d - 1].wait_recv()
    low[...] = mid[part(b, ROWS_B), :] + got_b[0] + got_b[1] + got_b[2]

    bigs, littles = [], []
    for d in range(1, NZ):
        zz = (z + d) % NZ
        bigs.append(send(low.at[part(zz, ROWS_Z), :], got_z.at[d - 1], along_z[d - 1]))
        littles.append(send(s_z.at[z], s_z.at[z], along_z[d - 1]))
    for d in range(1, NZ):
        littles[d - 1].wait_recv()
    s_all = ((s_z[0] + s_z[1]) + (s_z[2] + s_z[3])) + ((s_z[4] + s_z[5]) + (s_z[6] + s_z[7]))
    s_sum[:, part(a, SLICE)] = s_all
    final = low[part(z, ROWS_Z), :]
    for d in range(1, NZ):
        bigs[d - 1].wait_recv()
        final = final + got_z[d - 1]

    base_b = a * ROWS_A + b * ROWS_B
    mine = pl.ds(pl.multiple_of(base_b + z * ROWS_Z, ROWS_Z), ROWS_Z)
    half_out = big_out.at[core]
    half_out[mine, :] = final
    bigs = [send(half_out.at[mine, :], half_out.at[mine, :], peer) for peer in along_z]
    littles = [
        send(s_sum.at[:, part(a, SLICE)], s_sum.at[:, part(a, SLICE)], peer) for peer in along_a
    ]
    for copy in bigs:
        copy.wait_recv()
    rows_b = pl.ds(pl.multiple_of(base_b, ROWS_B), ROWS_B)
    bigs = [send(half_out.at[rows_b, :], half_out.at[rows_b, :], peer) for peer in along_b]
    for copy in littles:
        copy.wait_recv()
    small_out[core] = s_sum[...]
    little = send(small_out.at[core], small_out.at[core], partner)
    for copy in bigs:
        copy.wait_recv()
    rows_a = part(a, ROWS_A)
    bigs = [send(half_out.at[rows_a, :], half_out.at[rows_a, :], peer) for peer in along_a]
    for copy in bigs:
        copy.wait_recv()
    big = send(half_out, half_out, partner)
    little.wait_recv()
    big.wait_recv()
    for copy in started:
        copy.wait_send()


SENDS = 2 + 2 * (NX - 1) + 2 * (NY - 1) + 2 * (NZ - 1) + (NZ - 1) + (NX - 1) + (NY - 1) + (NX - 1) + 2


def sum_gradients(big, small):
    f32 = jnp.float32
    vmem = pl.BlockSpec(memory_space=pltpu.VMEM)
    return pl.pallas_call(
        sum_kernel,
        in_specs=[vmem, vmem],
        out_specs=[vmem, vmem],
        out_shape=[
            jax.ShapeDtypeStruct((NC, WIDE, HALF), f32),
            jax.ShapeDtypeStruct((NC, SMALL, HALF), f32),
        ],
        scratch_shapes=[
            pltpu.VMEM((WIDE, HALF), f32),
            pltpu.VMEM((WIDE, HALF), f32),
            pltpu.VMEM((NX - 1, ROWS_A, HALF), f32),
            pltpu.VMEM((ROWS_A, HALF), f32),
            pltpu.VMEM((NY - 1, ROWS_B, HALF), f32),
            pltpu.VMEM((ROWS_B, HALF), f32),
            pltpu.VMEM((NZ - 1, ROWS_Z, HALF), f32),
            pltpu.VMEM((SMALL, HALF), f32),
            pltpu.VMEM((NX - 1, SMALL, SLICE), f32),
            pltpu.VMEM((NY, SMALL, SLICE), f32),
            pltpu.VMEM((NZ, SMALL, SLICE), f32),
            pltpu.VMEM((SMALL, HALF), f32),
            pltpu.SemaphoreType.DMA((SENDS,)),
            pltpu.SemaphoreType.DMA((SENDS,)),
        ],
        compiler_params=pltpu.CompilerParams(collective_id=1, has_side_effects=True),
        name="gradients",
    )(big, small)


def features(set_rows):
    count = set_rows.shape[0]
    tenors, log_strike = strike_grid()
    scaled = set_rows * jnp.array([4.0, 1.0, 1.0, 20.0], dtype=jnp.float32)
    per_pair = jnp.stack([4.0 * log_strike.reshape(PAIRS), jnp.repeat(tenors, STRIKES)], axis=1)
    left = jnp.broadcast_to(scaled[:, None, :], (count, PAIRS, 4))
    right = jnp.broadcast_to(per_pair[None], (count, PAIRS, 2))
    return jnp.concatenate([left, right], axis=2).reshape(count * PAIRS, 6).astype(jnp.bfloat16)


def silu_slope(value):
    logistic = jax.nn.sigmoid(value)
    return logistic * (1.0 + value * (1.0 - logistic))


def contract_rows(left, right):
    return lax.dot_general(
        left, right, (((0,), (0,)), ((), ())), preferred_element_type=jnp.float32
    )


def local_terms(inputs, target, w_in, b_in, w_mid, b_mid, w_out, b_out, inv_sets):
    raw_in = jnp.dot(inputs, w_in, preferred_element_type=jnp.float32) + b_in
    hidden_in = jax.nn.silu(raw_in).astype(jnp.bfloat16)
    raw_mid = jnp.dot(hidden_in, w_mid, preferred_element_type=jnp.float32) + b_mid
    hidden_mid = jax.nn.silu(raw_mid).astype(jnp.bfloat16)
    predicted = jnp.dot(hidden_mid, w_out, preferred_element_type=jnp.float32) + b_out[0]
    slope = (predicted - target) * inv_sets
    grad_out = jnp.sum(hidden_mid.astype(jnp.float32) * slope[:, None], axis=0)
    grad_bout = jnp.sum(slope, keepdims=True)
    delta_mid = (slope[:, None] * w_out.astype(jnp.float32)[None, :] * silu_slope(raw_mid)).astype(
        jnp.bfloat16
    )
    grad_bmid = jnp.sum(delta_mid.astype(jnp.float32), axis=0)
    backward = lax.dot_general(
        delta_mid, w_mid, (((1,), (1,)), ((), ())), preferred_element_type=jnp.float32
    )
    delta_in = (backward * silu_slope(raw_in)).astype(jnp.bfloat16)
    grad_in = contract_rows(inputs, delta_in)
    grad_bin = jnp.sum(delta_in.astype(jnp.float32), axis=0)
    return ((grad_in, grad_bin, grad_bmid, grad_out, grad_bout), hidden_in, delta_mid)


def directions(grad_w, grad_b):
    entries = grad_w.size + grad_b.size
    mean_square = (jnp.sum(grad_w * grad_w) + jnp.sum(grad_b * grad_b)) / entries
    factor = lax.rsqrt(mean_square + EPSILON)
    return (grad_w * factor, grad_b * factor)


def on_device(params, increments, w_in, b_in, w_mid, b_mid, w_out, b_out):
    devices = lax.axis_size("paths")
    total_paths = increments.shape[2] * devices
    set_count = params.shape[0]
    owner = lax.axis_index("paths")
    prices = price_sums(params, increments)[:, :PAIRS] / total_paths
    own_params = lax.dynamic_slice_in_dim(params, owner * OWN, OWN, 0)
    small, hidden_in, delta_mid = local_terms(
        features(own_params),
        prices.reshape(-1),
        w_in,
        b_in,
        w_mid,
        b_mid,
        w_out,
        b_out,
        1.0 / set_count,
    )
    grad_mid = contract_rows(hidden_in, delta_mid)
    pad_out = jnp.pad(small[4], (0, WIDE - 1))
    packed = jnp.concatenate(
        [small[0], jnp.stack([small[1], small[2], small[3], pad_out]), jnp.zeros((6, WIDE), jnp.float32)]
    )
    big, little = sum_gradients(grad_mid, packed)
    grad_mid = jnp.concatenate([big[0], big[1]], axis=1)
    little = jnp.concatenate([little[0], little[1]], axis=1)
    direction_w_mid, direction_b_mid = directions(grad_mid, little[7])
    direction_w_in, direction_b_in = directions(little[:6], little[6])
    direction_w_out, direction_b_out = directions(little[8], little[9, :1])
    return (
        prices,
        direction_w_in,
        direction_b_in,
        direction_w_mid,
        direction_b_mid,
        direction_w_out,
        direction_b_out,
    )


def solution(mesh):
    in_specs = (P(), P(None, None, "paths"), P(), P(), P(), P(), P(), P())
    out_specs = (P("paths", None), P(), P(), P(), P(), P(), P())
    return jax.shard_map(
        on_device, mesh=mesh, in_specs=in_specs, out_specs=out_specs, check_vma=False
    )
```

time: 807 us -> 175 us (0.22)
  waiting for transfers between devices: 425 us -> 0 us
  matrix products: 163 us -> 12.7 us
  Pallas kernels: 0 us -> 115 us
  blocking collectives: 79.2 us -> 0 us
  other arithmetic: 72 us -> 23.4 us
  local copies, waits for them, and re-layouts: 39.8 us -> 13.2 us
  between operations: 21.2 us -> 8.05 us
    psum x2 -> x0, waiting for transfers between devices: 425 us -> none  [the longest x1 250 us: on_device(): summed = lax.psum(every_set, 'paths')]
    dot_general x16 -> x0, matrix products: 148 us -> none  [payoff_sums(): jnp.dot(kernel.reshape(count * STEPS, STEPS), increments[0], preferred_el...]
    pallas_call x0 -> x2, Pallas kernels: none -> 115 us  [the longest x1 70.1 us: sum_gradients(): pl.pallas_call(sum_kernel, in_specs=[vmem, vmem], out_specs=[vmem, vmem],...]
    psum x1 -> x0, blocking collectives: 79.2 us -> none  [on_device(): lax.psum((small[0], small[1], small[2], small[3], small[4], grad_mid), 'p...]
    reduce_sum x17 -> x0, other arithmetic: 26.8 us -> none  [the longest x16 26.2 us: payoff_sums(): return jnp.sum(gains, axis=3).reshape(count, PAIRS)]
    mul x48 -> x1, other arithmetic: 14.1 us -> 0.01 us  [set_operands(): times = lag * delta_t]
    dynamic_update_slice x16 -> x0, local copies, waits for them, and re-layouts: 10 us -> none  [evolve(): sums = lax.map(lambda group: payoff_sums(group, increments), groups)]
  transfers between devices with their start and end apart: 2 -> 0, of which waited for: 2 -> 0; matrix products, arithmetic and copies ran while one was open for 2% -> 0% of each run, Pallas kernels for 0% -> 0%
where the time goes in v1:
time: 175 us; the launch traced here: 172 us
  Pallas kernels  115 us (66%)
  other arithmetic  23.4 us (13%)
  local copies, waits for them, and re-layouts  13.2 us (8%)
  matrix products  12.7 us (7%)
  between operations  8.05 us (5%)
    pallas_call x1, Pallas kernels, sum_gradients(): pl.pallas_call(sum_kernel, in_specs=[vmem, vmem], out_specs=[vmem, vmem],...  70.1 us
    pallas_call x1, Pallas kernels, price_sums(): pl.pallas_call(prices_kernel, grid=(BLOCKS,), in_specs=[pl.BlockSpec((BLO...  44.9 us
    mul x5, other arithmetic, directions(): return (grad_w * factor, grad_b * factor)  7.37 us
    another operation x4, other arithmetic  7.18 us
    dot_general x2, matrix products, contract_rows(): lax.dot_general(left, right, (((0,), (0,)), ((), ())), preferred_element_...  6.63 us

profile of v1, /device:TPU:1, one launch (start us, length us, event | category | flops | bytes accessed | tf_op | source)
XLA Modules:
  0.0 172.5 jit_solution(14074691782556032684)
XLA Ops:
  0.7 1.7 reshape.109
  2.8 0.7 multiply_bitcast_fusion
  3.5 4.7 %fusion.1 = (bf16[2048,64]{1,0:T(8,128)(2,1)S(1)}, bf16[2048,64]{1,0:T(8,128)(2,1)S(1)}, bf16[2048,64]{1,0:T(8,128)(2,1)S(1)}) fusion(f32[2048]{0:T(1024)S(1)} %bitcast.68, f32[2048]{0:T(1024)S(1)} %bitcast.67, f32[64]{0:T(128)S(1)} %broadcast_add_fusion.1, f32[2048]{0:T(1024)S(1)} %bitcast.69, f32[64]{0:T(128)S(1)} %get-tuple-element.51, ...), kind=kLoop, calls=%fused_computation.19 | loop fusion | flops 1703936 | bytes 852864 | tf_op jit(solution)/shard_map/convert.2
  8.3 1.7 fusion.8
  10.0 1.7 pad_maximum_fusion.1.rows_ref
  11.7 1.3 broadcast_in_dim.111.ratio_ref
  13.0 44.9 %prices.1 = f32[8,128]{1,0:T(8,128)} custom-call(bf16[2048,256]{1,0:T(8,128)(2,1)} %pad_maximum_fusion.1.rows_ref, f32[2048,128]{1,0:T(8,128)} %broadcast_in_dim.111.ratio_ref, f32[1,2048]{1,0:T(1,128)} %get-tuple-element.31.scale_ref, bf16[2,64,128]{2,1,0:T(8,128)(2,1)} %inc_ref.1), custom_call_target="tpu_custom_call" | custom-call | tf_op jit(solution)/shard_map/prices/pallas_call | solution.py:252
  57.9 0.7 slice_multiply_fusion.2
  58.7 0.8 multiply_convert_fusion.4
  60.7 2.1 %multiply_convert_fusion.2 = (bf16[704,1024]{1,0:T(8,128)(2,1)S(1)}, f32[704,1024]{1,0:T(8,128)S(1)}) fusion(f32[1024]{0:T(1024)S(1)} %copy-done.7, bf16[1024,1024]{1,0:T(8,128)(2,1)S(1)} %copy-done, f32[704,1024]{1,0:T(8,128)S(1)} %fusion.26, f32[1024]{0:T(1024)S(1)} %copy-done.10), kind=kOutput, calls=%fused_computation.8 | convolution fusion | flops 1485045760 | bytes 9314304 | tf_op jit(solution)/shard_map/dot_general | solution.py:485
  64.6 2.2 %convert_reduce_fusion = (f32[1024]{0:T(1024)S(1)}, bf16[704,1024]{1,0:T(8,128)(2,1)S(1)}, f32[1024]{0:T(1024)}) fusion(f32[704,1024]{1,0:T(8,128)S(1)} %get-tuple-element.47, f32[1024]{0:T(1024)S(1)} %copy-done.8, f32[1024]{0:T(1024)S(1)} %convert_element_type.34, f32[704]{0:T(1024)S(1)} %get-tuple-element.18, bf16[704,1024]{1,0:T(8,128)(2,1)S(1)} %get-tuple-element.46), kind=kLoop, calls=%fused_computation.4 | loop fusion | flops 11532288 | bytes 5786368 | tf_op jit(solution)/shard_map/reduce_sum | solution.py:494
  66.8 2.9 %convert_reduce_fusion.1 = (f32[1024]{0:T(1024)}, bf16[704,1024]{1,0:T(8,128)(2,1)S(1)}) fusion(f32[704,1024]{1,0:T(8,128)S(1)} %fusion.26, f32[1024]{0:T(1024)S(1)} %copy-done.11, bf16[704,1024]{1,0:T(8,128)(2,1)S(1)} %get-tuple-element.20, bf16[1024,1024]{1,0:T(8,128)(2,1)S(1)} %copy-done), kind=kOutput, calls=%fused_computation.5 | convolution fusion | flops 1485044736 | bytes 7872512 | tf_op jit(solution)/shard_map/dot_general | solution.py:495
  69.7 0.9 fusion.27
  70.6 0.6 pad.4
  71.3 0.6 broadcast_in_dim.116
  71.9 2.8 %concatenate.23.small_ref = f32[16,1024]{1,0:T(8,128)} concatenate(f32[6,1024]{1,0:T(8,128)} %fusion.27, f32[1,1024]{1,0:T(1,128)} %bitcast.74, f32[1,1024]{1,0:T(1,128)S(1)} %bitcast.71, f32[1,1024]{1,0:T(1,128)} %bitcast.72, f32[1,1024]{1,0:T(1,128)S(1)} %bitcast.73, f32[6,1024]{1,0:T(8,128)} %broadcast_in_dim.116), dimensions={0} | concatenate | bytes 131072 | tf_op jit(solution)/shard_map/concatenate | solution.py:531
  74.7 5.7 %fusion.19.big_ref = f32[1024,1024]{1,0:T(8,128)} fusion(bf16[704,1024]{1,0:T(8,128)(2,1)S(1)} %get-tuple-element.20, f32[704,1024]{1,0:T(8,128)} %copy-done.3, f32[1024]{0:T(1024)} %param.12), kind=kOutput, calls=%fused_computation.84 | convolution fusion | flops 1480720384 | bytes 8523776 | tf_op jit(solution)/shard_map/dot_general | solution.py:477
  80.4 70.1 %gradients.1 = (f32[2,1024,512]{2,1,0:T(8,128)}, f32[2,16,512]{2,1,0:T(8,128)}) custom-call(f32[1024,1024]{1,0:T(8,128)} %fusion.19.big_ref, f32[16,1024]{1,0:T(8,128)} %concatenate.23.small_ref), custom_call_target="tpu_custom_call" | custom-call | tf_op jit(solution)/shard_map/gradients/pallas_call | solution.py:432
  150.5 0.8 slice_bitcast_fusion.3
  151.3 0.6 multiply_reduce_fusion.3
  155.6 2.7 %slice_bitcast_fusion.1 = (f32[1024,512]{1,0:T(8,128)S(1)}, f32[1024,512]{1,0:T(8,128)S(1)}) fusion(f32[2,1024,512]{2,1,0:T(8,128)} %get-tuple-element.10), kind=kLoop, calls=%fused_computation.13 | loop fusion | bytes 8388608 | tf_op jit(solution)/shard_map/squeeze | solution.py:535
  158.3 1.3 copy-done.1
  159.6 1.7 multiply_reduce_fusion
  163.2 5.0 %fusion = f32[1024,1024]{1,0:T(8,128)} fusion(f32[1024,512]{1,0:T(8,128)} %copy-done.2, f32[1024,512]{1,0:T(8,128)} %copy-done.1, f32[]{:T(128)S(6)} %rsqrt.10), kind=kLoop, calls=%fused_computation.2 | loop fusion | flops 2097152 | bytes 8388612 | tf_op jit(solution)/shard_map/mul | solution.py:508
  (55 shorter events, 6.3 us)
Async XLA Ops:
  0.6 60.0 %copy-start = (bf16[1024,1024]{1,0:T(8,128)(2,1)S(1)}, bf16[1024,1024]{1,0:T(8,128)(2,1)}, u32[]{:S(2)}) copy-start(bf16[1024,1024]{1,0:T(8,128)(2,1)} %param.13) | copy-start | bytes 6291460
  10.0 48.7 %copy-start.9 = (f32[4]{0:T(128)S(1)}, f32[4]{0:T(128)}, u32[]{:S(2)}) copy-start(f32[4]{0:T(128)} %constant.101.clone) | copy-start | bytes 52
  10.0 50.1 %copy-start.4 = (bf16[6,1024]{1,0:T(8,128)(2,1)S(1)}, bf16[6,1024]{1,0:T(8,128)(2,1)}, u32[]{:S(2)}) copy-start(bf16[6,1024]{1,0:T(8,128)(2,1)} %param.11) | copy-start | bytes 36868
  11.7 49.0 %copy-start.7 = (f32[1024]{0:T(1024)S(1)}, f32[1024]{0:T(1024)}, u32[]{:S(2)}) copy-start(f32[1024]{0:T(1024)} %param.14) | copy-start | bytes 12292
  11.7 49.0 %copy-start.10 = (f32[1024]{0:T(1024)S(1)}, f32[1024]{0:T(1024)}, u32[]{:S(2)}) copy-start(f32[1024]{0:T(1024)} %param.12) | copy-start | bytes 12292
  58.6 1.3 copy-start.5
  60.7 6.1 %copy-start.3 = (f32[704,1024]{1,0:T(8,128)}, f32[704,1024]{1,0:T(8,128)S(1)}, u32[]{:S(2)}) copy-start(f32[704,1024]{1,0:T(8,128)S(1)} %fusion.26) | copy-start | bytes 8650756
  60.7 2.1 %copy-start.6 = (bf16[1024]{0:T(1024)(128)(2,1)S(1)}, bf16[1024]{0:T(1024)(128)(2,1)}, u32[]{:S(2)}) copy-start(bf16[1024]{0:T(1024)(128)(2,1)} %param.15) | copy-start | bytes 6148
  60.7 3.9 %copy-start.8 = (f32[1024]{0:T(1024)S(1)}, f32[1024]{0:T(1024)}, u32[]{:S(2)}) copy-start(f32[1024]{0:T(1024)} %param.14) | copy-start | bytes 12292
  64.6 2.2 %copy-start.11 = (f32[1024]{0:T(1024)S(1)}, f32[1024]{0:T(1024)}, u32[]{:S(2)}) copy-start(f32[1024]{0:T(1024)} %param.12) | copy-start | bytes 12292
  158.3 1.3 copy-start.1
  158.3 3.0 %copy-start.2 = (f32[1024,512]{1,0:T(8,128)}, f32[1024,512]{1,0:T(8,128)S(1)}, u32[]{:S(2)}) copy-start(f32[1024,512]{1,0:T(8,128)S(1)} %get-tuple-element.24) | copy-start | bytes 6291460

commit v2 on v1

--- a/solution.py
+++ b/solution.py
@@ -2,6 +2,7 @@
 
 import jax
 import jax.numpy as jnp
+import numpy as np
 from jax import lax
 from jax.experimental import pallas as pl
 from jax.experimental.pallas import tpu as pltpu
@@ -17,14 +18,9 @@
 OWN = 8
 BLOCK = NY * NZ * OWN
 BLOCKS = NX * NC
+SETS = 2048
+TOTAL_PATHS = 32768
 MESH = pl.DeviceIdType.MESH
-
-
-def strike_grid():
-    tenors = (jnp.arange(MATS, dtype=jnp.float32) + 1.0) / MATS
-    offsets = jnp.arange(STRIKES, dtype=jnp.float32) - (STRIKES - 1) / 2.0
-    log_strike = 0.05 * offsets[None, :] * jnp.sqrt(tenors)[:, None]
-    return (tenors, log_strike)
 
 
 def strike_values():
@@ -32,10 +28,6 @@
         [math.exp(0.05 * (j - 5) * math.sqrt((m + 1) / MATS)) for j in range(STRIKES)]
         for m in range(MATS)
     ]
-
-
-def round_bf16(x):
-    return lax.reduce_precision(x, 8, 7)
 
 
 def coords(index):
@@ -50,41 +42,48 @@
     return ((x * NY + y) * NZ + z) * NC + core
 
 
-def set_operands(params):
-    hurst, vol, correl, forward = (params[:, k : k + 1] for k in range(4))
-    delta_t = 1.0 / STEPS
-    lag = jnp.arange(STEPS, dtype=jnp.float32)[None, :]
-    high = jnp.maximum(lag, 1.0)
+def lag_tables():
+    lag = np.tile(np.arange(STEPS, dtype=np.float64), 2)
+    table = np.zeros((8, 128), np.float32)
+    table[0] = np.log2(np.maximum(lag, 1.0))
+    table[1] = np.log2(np.maximum(lag - 1.0, 1.0))
+    table[2] = np.log2(np.maximum(lag, 1.0) / STEPS)
+    return table
+
+
+def set_operands(sets, lag_ref, rows, ratio, scale):
+    f32, bf16 = jnp.float32, jnp.bfloat16
+    shape = (sets.shape[0], 128)
+    hurst, vol, correl, forward = (
+        jnp.broadcast_to(sets[:, k : k + 1], shape) for k in range(4)
+    )
+    lane = lax.broadcasted_iota(jnp.int32, shape, 1)
+    upper = lane >= STEPS
+    lag = jnp.where(upper, lane - STEPS, lane)
     expo = hurst + 0.5
-    powers = jnp.power(high, expo) - jnp.power(high - 1.0, expo)
-    front = jnp.sqrt(2.0 * hurst) * jnp.power(delta_t, hurst) / (hurst + 0.5)
-    kern = round_bf16(jnp.where(lag >= 1.0, powers * front, 0.0))
+    late = jnp.where(lag >= 2, jnp.exp2(expo * lag_ref[1:2, :]), 0.0)
+    powers = jnp.exp2(expo * lag_ref[0:1, :]) - late
+    front = jnp.sqrt(2.0 * hurst) * jnp.exp2(-6.0 * hurst) / expo
+    kern = jnp.where(lag >= 1, powers * front, 0.0).astype(bf16).astype(f32)
     half = (0.5 * LOG2E) * vol
     weight = kern * half
-    times = lag * delta_t
-    comp = -0.5 * vol * half * jnp.power(times, 2.0 * hurst)
-    mix = jnp.sqrt(1.0 - correl * correl)
-    const = 0.5 * jnp.log2(forward * delta_t) - 1.0 - jnp.log2(mix)
-    w_hi = round_bf16(weight)
-    w_lo = round_bf16(weight - w_hi)
-    c_hi = round_bf16(comp)
-    c_lo = round_bf16(comp - c_hi)
-    k_hi = round_bf16(const)
-    k_lo = round_bf16(const - k_hi)
-    k_ll = const - k_hi - k_lo
-    first = lag < 0.5
-    rows = jnp.concatenate(
-        [
-            jnp.where(first, k_hi, w_hi),
-            jnp.where(first, k_lo, w_lo),
-            jnp.where(first, k_ll, c_hi),
-            jnp.where(first, 0.0, c_lo),
-        ],
-        axis=1,
-    ).astype(jnp.bfloat16)
-    ratio = jnp.broadcast_to(correl / mix, (params.shape[0], 128))
-    scale = (2.0 * LOG2E) * (mix * mix)
-    return rows, ratio, scale.reshape(1, -1)
+    comp = (-0.5 * vol * half) * jnp.exp2((2.0 * hurst) * lag_ref[2:3, :])
+    rest = 1.0 - correl * correl
+    const = (0.5 * LOG2E) * jnp.log(forward * (1.0 / STEPS) / rest) - 1.0
+    w_hi = weight.astype(bf16).astype(f32)
+    c_hi = comp.astype(bf16).astype(f32)
+    k_hi = const.astype(bf16).astype(f32)
+    k_rest = const - k_hi
+    k_lo = k_rest.astype(bf16).astype(f32)
+    first = lag == 0
+    kern_row = jnp.where(first, jnp.where(upper, k_lo, k_hi), jnp.where(upper, weight - w_hi, w_hi))
+    comp_row = jnp.where(
+        first, jnp.where(upper, 0.0, k_rest - k_lo), jnp.where(upper, comp - c_hi, c_hi)
+    )
+    rows[:, 0:128] = kern_row.astype(bf16)
+    rows[:, 128:256] = comp_row.astype(bf16)
+    ratio[...] = correl * lax.rsqrt(rest)
+    scale[...] = (2.0 * LOG2E) * rest
 
 
 def price_peers(x, y, z, core):
@@ -99,11 +98,15 @@
 
 
 def prices_kernel(
+    params_ref,
+    lag_ref,
+    inc_ref,
+    out_ref,
+    own_ref,
+    sets,
     rows_ref,
     ratio_ref,
     scale_ref,
-    inc_ref,
-    out_ref,
     noise,
     table,
     walk,
@@ -128,6 +131,11 @@
         barrier = pltpu.get_barrier_semaphore()
         for peer in blocks + along_y + along_z:
             pl.semaphore_signal(barrier, inc=1, device_id=(peer,), device_id_type=MESH)
+        for k in range(NX * NY):
+            some = params_ref[:, pl.ds(k * 128, 128)]
+            some = jnp.concatenate([some, jnp.zeros((120, 128), jnp.float32)], axis=0).T
+            sets[k // NY, pl.ds((k % NY) * NZ, NZ)] = some.reshape(NZ, NC, OWN, 128)
+        own_ref[...] = sets[x, y * NZ + z, core]
         noise[0] = inc_ref[0].astype(jnp.float32)
         noise[1] = inc_ref[1].astype(jnp.float32)
         part[...] = jnp.zeros_like(part)
@@ -149,8 +157,10 @@
             table[i // 2, pl.ds(3 * STEPS, STEPS), cols] = hot_lo
 
     strikes = strike_values()
+    other = (x * NC + core + 1 + step) % BLOCKS
+    block = sets[other // NC, :, other % NC].reshape(BLOCK, 128)
+    set_operands(block, lag_ref, rows_ref, ratio_ref, scale_ref)
     walk[...] = jnp.zeros_like(walk)
-    scale = scale_ref[...]
     for m in range(MATS):
         for q in range(4):
             pair = jnp.dot(
@@ -161,7 +171,7 @@
                 vol = jnp.exp2(pair[:, h * 128 : (h + 1) * 128])
                 shock = ratio_ref[...] * noise[0, pl.ds(i, 1), :] + noise[1, pl.ds(i, 1), :]
                 walk[...] += vol * (shock - vol)
-        spot = jnp.exp2(walk[...].T * scale)
+        spot = jnp.exp2((walk[...] * scale_ref[...]).T)
         for j in range(STRIKES):
             k = strikes[m][j]
             top = jnp.sum(jnp.maximum(spot, k).reshape(16, 8, BLOCK), axis=0)
@@ -242,33 +252,31 @@
 
 
 def price_sums(params, increments):
-    index = lax.axis_index("paths")
-    x, y, z, core = coords(index)
-    order = params.reshape(NX, NY, NZ, NC, OWN, 4).transpose(0, 3, 1, 2, 4, 5)
-    order = order.reshape(BLOCKS, BLOCK, 4)
-    order = jnp.concatenate([order, order], axis=0)
-    order = lax.dynamic_slice_in_dim(order, x * NC + core + 1, BLOCKS, 0)
-    rows, ratio, scale = set_operands(order.reshape(BLOCKS * BLOCK, 4))
+    f32 = jnp.float32
+    own = jax.ShapeDtypeStruct((OWN, 128), f32)
     return pl.pallas_call(
         prices_kernel,
         grid=(BLOCKS,),
         in_specs=[
-            pl.BlockSpec((BLOCK, 256), lambda b: (b, 0)),
-            pl.BlockSpec((BLOCK, 128), lambda b: (b, 0)),
-            pl.BlockSpec((1, BLOCK), lambda b: (0, b)),
+            pl.BlockSpec((8, BLOCKS * BLOCK), lambda b: (0, 0)),
+            pl.BlockSpec((8, 128), lambda b: (0, 0)),
             pl.BlockSpec((2, STEPS, 128), lambda b: (0, 0, 0)),
         ],
-        out_specs=pl.BlockSpec((OWN, 128), lambda b: (0, 0)),
-        out_shape=jax.ShapeDtypeStruct((OWN, 128), jnp.float32),
+        out_specs=[pl.BlockSpec((OWN, 128), lambda b: (0, 0))] * 2,
+        out_shape=[own, own],
         scratch_shapes=[
-            pltpu.VMEM((2, STEPS, 128), jnp.float32),
+            pltpu.VMEM((NX, NY * NZ, NC, OWN, 128), f32),
+            pltpu.VMEM((BLOCK, 256), jnp.bfloat16),
+            pltpu.VMEM((BLOCK, 128), f32),
+            pltpu.VMEM((BLOCK, 128), f32),
+            pltpu.VMEM((2, STEPS, 128), f32),
             pltpu.VMEM((STEPS // 2, 256, 256), jnp.bfloat16),
-            pltpu.VMEM((BLOCK, 128), jnp.float32),
-            pltpu.VMEM((128, BLOCK), jnp.float32),
-            pltpu.VMEM((BLOCKS, BLOCK, 128), jnp.float32),
-            pltpu.VMEM((BLOCKS - 1, BLOCK, 128), jnp.float32),
-            pltpu.VMEM((NY, NZ * OWN, 128), jnp.float32),
-            pltpu.VMEM((NZ, OWN, 128), jnp.float32),
+            pltpu.VMEM((BLOCK, 128), f32),
+            pltpu.VMEM((128, BLOCK), f32),
+            pltpu.VMEM((BLOCKS, BLOCK, 128), f32),
+            pltpu.VMEM((BLOCKS - 1, BLOCK, 128), f32),
+            pltpu.VMEM((NY, NZ * OWN, 128), f32),
+            pltpu.VMEM((NZ, OWN, 128), f32),
             pltpu.SemaphoreType.DMA((BLOCKS,)),
             pltpu.SemaphoreType.DMA((BLOCKS,)),
             pltpu.SemaphoreType.DMA((NY,)),
@@ -278,7 +286,7 @@
         ],
         compiler_params=pltpu.CompilerParams(collective_id=0, has_side_effects=True),
         name="prices",
-    )(rows, ratio, scale, increments)
+    )(jnp.pad(params.T, ((0, 4), (0, 0))), jnp.asarray(lag_tables()), increments)
 
 
 WIDE = 1024
@@ -458,94 +466,173 @@
     )(big, small)
 
 
-def features(set_rows):
-    count = set_rows.shape[0]
-    tenors, log_strike = strike_grid()
-    scaled = set_rows * jnp.array([4.0, 1.0, 1.0, 20.0], dtype=jnp.float32)
-    per_pair = jnp.stack([4.0 * log_strike.reshape(PAIRS), jnp.repeat(tenors, STRIKES)], axis=1)
-    left = jnp.broadcast_to(scaled[:, None, :], (count, PAIRS, 4))
-    right = jnp.broadcast_to(per_pair[None], (count, PAIRS, 2))
-    return jnp.concatenate([left, right], axis=2).reshape(count * PAIRS, 6).astype(jnp.bfloat16)
-
-
-def silu_slope(value):
-    logistic = jax.nn.sigmoid(value)
-    return logistic * (1.0 + value * (1.0 - logistic))
-
-
-def contract_rows(left, right):
-    return lax.dot_general(
-        left, right, (((0,), (0,)), ((), ())), preferred_element_type=jnp.float32
+ROWS = PAIRS * OWN
+CHUNK = ROWS // 4
+
+
+def pair_table():
+    tenors = (np.arange(MATS, dtype=np.float32) + np.float32(1.0)) / np.float32(MATS)
+    offsets = np.arange(STRIKES, dtype=np.float32) - np.float32((STRIKES - 1) / 2.0)
+    log_strike = np.float32(0.05) * offsets[None, :] * np.sqrt(tenors)[:, None]
+    table = np.zeros((PAIRS, 128), np.float32)
+    table[:, 4] = np.float32(4.0) * log_strike.reshape(PAIRS)
+    table[:, 5] = np.repeat(tenors, STRIKES)
+    table[:, 6] = 1.0
+    return table
+
+
+def network_kernel(
+    sets_ref,
+    table_ref,
+    prices_ref,
+    w_in_ref,
+    b_in_ref,
+    w_mid_ref,
+    b_mid_ref,
+    w_out_ref,
+    b_out_ref,
+    prices_out,
+    big_ref,
+    small_ref,
+    feats,
+    hid_in,
+    slope_in,
+    delta_mid,
+    delta_in,
+):
+    f32, bf16 = jnp.float32, jnp.bfloat16
+    pairs = CHUNK // OWN
+    lane = lax.broadcasted_iota(jnp.int32, (OWN, 128), 1)
+    factor = jnp.where(lane == 0, 4.0, jnp.where(lane == 3, 20.0, 1.0))
+    scaled = (sets_ref[...] * factor)[None, :, :]
+    prices = prices_ref[:, :PAIRS] / TOTAL_PATHS
+    prices_out[...] = prices
+    w_out = w_out_ref[...].astype(f32)
+    g_out = jnp.zeros((8, WIDE), f32)
+    g_bmid = jnp.zeros((8, WIDE), f32)
+    g_bin = jnp.zeros((8, WIDE), f32)
+    g_bout = jnp.zeros((8, 1), f32)
+    for c in range(ROWS // CHUNK):
+        rows = pl.ds(c * CHUNK, CHUNK)
+        table = table_ref[pl.ds(c * pairs, pairs), :]
+        x = (table[:, None, :] + scaled).reshape(CHUNK, 128).astype(bf16)
+        feats[rows, :] = x
+        raw = jnp.dot(x[:, :6], w_in_ref[...], preferred_element_type=f32) + b_in_ref[...]
+        g = jax.nn.sigmoid(raw)
+        hid = (raw * g).astype(bf16)
+        hid_in[rows, :] = hid
+        slope_in[rows, :] = g * (1.0 + raw * (1.0 - g))
+        raw = jnp.dot(hid, w_mid_ref[...], preferred_element_type=f32) + b_mid_ref[...]
+        g = jax.nn.sigmoid(raw)
+        mid = (raw * g).astype(bf16).astype(f32)
+        pred = jnp.sum(mid * w_out, axis=1, keepdims=True) + b_out_ref[0, 0]
+        target = jnp.concatenate(
+            [prices[:, k : k + 1] for k in range(c * pairs, (c + 1) * pairs)], axis=0
+        )
+        slope = (pred - target) * (1.0 / SETS)
+        g_bout = g_bout + jnp.sum(slope.reshape(pairs, 8, 1), axis=0)
+        g_out = g_out + jnp.sum((mid * slope).reshape(pairs, 8, WIDE), axis=0)
+        delta = (slope * w_out * (g * (1.0 + raw * (1.0 - g)))).astype(bf16)
+        delta_mid[rows, :] = delta
+        g_bmid = g_bmid + jnp.sum(delta.astype(f32).reshape(pairs, 8, WIDE), axis=0)
+        back = lax.dot_general(
+            delta, w_mid_ref[...], (((1,), (1,)), ((), ())), preferred_element_type=f32
+        )
+        inner = (back * slope_in[rows, :]).astype(bf16)
+        delta_in[rows, :] = inner
+        g_bin = g_bin + jnp.sum(inner.astype(f32).reshape(pairs, 8, WIDE), axis=0)
+    small_ref[pl.ds(0, 8), :] = lax.dot_general(
+        feats[:, :8], delta_in[...], (((0,), (0,)), ((), ())), preferred_element_type=f32
     )
-
-
-def local_terms(inputs, target, w_in, b_in, w_mid, b_mid, w_out, b_out, inv_sets):
-    raw_in = jnp.dot(inputs, w_in, preferred_element_type=jnp.float32) + b_in
-    hidden_in = jax.nn.silu(raw_in).astype(jnp.bfloat16)
-    raw_mid = jnp.dot(hidden_in, w_mid, preferred_element_type=jnp.float32) + b_mid
-    hidden_mid = jax.nn.silu(raw_mid).astype(jnp.bfloat16)
-    predicted = jnp.dot(hidden_mid, w_out, preferred_element_type=jnp.float32) + b_out[0]
-    slope = (predicted - target) * inv_sets
-    grad_out = jnp.sum(hidden_mid.astype(jnp.float32) * slope[:, None], axis=0)
-    grad_bout = jnp.sum(slope, keepdims=True)
-    delta_mid = (slope[:, None] * w_out.astype(jnp.float32)[None, :] * silu_slope(raw_mid)).astype(
-        jnp.bfloat16
+    small_ref[pl.ds(6, 1), :] = jnp.sum(g_bin, axis=0, keepdims=True)
+    small_ref[pl.ds(7, 1), :] = jnp.sum(g_bmid, axis=0, keepdims=True)
+    small_ref[pl.ds(8, 1), :] = jnp.sum(g_out, axis=0, keepdims=True)
+    small_ref[pl.ds(9, 1), :] = jnp.broadcast_to(jnp.sum(g_bout, axis=0, keepdims=True), (1, WIDE))
+    small_ref[pl.ds(10, 6), :] = jnp.zeros((6, WIDE), f32)
+    big_ref[...] = lax.dot_general(
+        hid_in[...], delta_mid[...], (((0,), (0,)), ((), ())), preferred_element_type=f32
     )
-    grad_bmid = jnp.sum(delta_mid.astype(jnp.float32), axis=0)
-    backward = lax.dot_general(
-        delta_mid, w_mid, (((1,), (1,)), ((), ())), preferred_element_type=jnp.float32
+
+
+def network(sets, prices, w_in, b_in, w_mid, b_mid, w_out, b_out):
+    f32, bf16 = jnp.float32, jnp.bfloat16
+    vmem = pl.BlockSpec(memory_space=pltpu.VMEM)
+    smem = pl.BlockSpec(memory_space=pltpu.SMEM)
+    return pl.pallas_call(
+        network_kernel,
+        in_specs=[vmem] * 8 + [smem],
+        out_specs=[vmem, vmem, vmem],
+        out_shape=[
+            jax.ShapeDtypeStruct((OWN, PAIRS), f32),
+            jax.ShapeDtypeStruct((WIDE, WIDE), f32),
+            jax.ShapeDtypeStruct((SMALL, WIDE), f32),
+        ],
+        scratch_shapes=[
+            pltpu.VMEM((ROWS, 128), bf16),
+            pltpu.VMEM((ROWS, WIDE), bf16),
+            pltpu.VMEM((ROWS, WIDE), f32),
+            pltpu.VMEM((ROWS, WIDE), bf16),
+            pltpu.VMEM((ROWS, WIDE), bf16),
+        ],
+        name="network",
+    )(
+        sets,
+        jnp.asarray(pair_table()),
+        prices,
+        w_in,
+        b_in.reshape(1, WIDE),
+        w_mid,
+        b_mid.reshape(1, WIDE),
+        w_out.reshape(1, WIDE),
+        b_out.reshape(1, 1),
     )
-    delta_in = (backward * silu_slope(raw_in)).astype(jnp.bfloat16)
-    grad_in = contract_rows(inputs, delta_in)
-    grad_bin = jnp.sum(delta_in.astype(jnp.float32), axis=0)
-    return ((grad_in, grad_bin, grad_bmid, grad_out, grad_bout), hidden_in, delta_mid)
-
-
-def directions(grad_w, grad_b):
-    entries = grad_w.size + grad_b.size
-    mean_square = (jnp.sum(grad_w * grad_w) + jnp.sum(grad_b * grad_b)) / entries
-    factor = lax.rsqrt(mean_square + EPSILON)
-    return (grad_w * factor, grad_b * factor)
+
+
+def finish_kernel(
+    big_ref, small_ref, w_in_out, b_in_out, w_mid_out, b_mid_out, w_out_out, b_out_out
+):
+    def factor(total, entries):
+        return lax.rsqrt(total * (1.0 / entries) + EPSILON)
+
+    def sumsq(value):
+        return jnp.sum(jnp.sum(value * value, axis=1, keepdims=True), axis=0, keepdims=True)
+
+    small = jnp.concatenate([small_ref[0], small_ref[1]], axis=1)
+    g_bout = small[9:10, 0:1]
+    s_mid = sumsq(small[7:8])
+    for k in range(8):
+        for c in range(NC):
+            s_mid = s_mid + sumsq(big_ref[c, pl.ds(k * 128, 128), :])
+    f_in = factor(sumsq(small[0:7]), 7 * WIDE)
+    f_mid = factor(s_mid, (WIDE + 1) * WIDE)
+    f_out = factor(sumsq(small[8:9]) + g_bout * g_bout, WIDE + 1)
+    w_in_out[...] = small[0:6] * f_in
+    b_in_out[...] = small[6:7] * f_in
+    b_mid_out[...] = small[7:8] * f_mid
+    w_out_out[...] = small[8:9] * f_out
+    b_out_out[...] = g_bout * f_out
+    for c in range(NC):
+        w_mid_out[:, pl.ds(c * HALF, HALF)] = big_ref[c] * f_mid
+
+
+def finish(big, small):
+    f32 = jnp.float32
+    vmem = pl.BlockSpec(memory_space=pltpu.VMEM)
+    shapes = [(6, WIDE), (1, WIDE), (WIDE, WIDE), (1, WIDE), (1, WIDE), (1, 1)]
+    w_in, b_in, w_mid, b_mid, w_out, b_out = pl.pallas_call(
+        finish_kernel,
+        in_specs=[vmem] * 2,
+        out_specs=[vmem] * 6,
+        out_shape=[jax.ShapeDtypeStruct(shape, f32) for shape in shapes],
+        name="finish",
+    )(big, small)
+    return w_in, b_in.reshape(WIDE), w_mid, b_mid.reshape(WIDE), w_out.reshape(WIDE), b_out.reshape(1)
 
 
 def on_device(params, increments, w_in, b_in, w_mid, b_mid, w_out, b_out):
-    devices = lax.axis_size("paths")
-    total_paths = increments.shape[2] * devices
-    set_count = params.shape[0]
-    owner = lax.axis_index("paths")
-    prices = price_sums(params, increments)[:, :PAIRS] / total_paths
-    own_params = lax.dynamic_slice_in_dim(params, owner * OWN, OWN, 0)
-    small, hidden_in, delta_mid = local_terms(
-        features(own_params),
-        prices.reshape(-1),
-        w_in,
-        b_in,
-        w_mid,
-        b_mid,
-        w_out,
-        b_out,
-        1.0 / set_count,
-    )
-    grad_mid = contract_rows(hidden_in, delta_mid)
-    pad_out = jnp.pad(small[4], (0, WIDE - 1))
-    packed = jnp.concatenate(
-        [small[0], jnp.stack([small[1], small[2], small[3], pad_out]), jnp.zeros((6, WIDE), jnp.float32)]
-    )
-    big, little = sum_gradients(grad_mid, packed)
-    grad_mid = jnp.concatenate([big[0], big[1]], axis=1)
-    little = jnp.concatenate([little[0], little[1]], axis=1)
-    direction_w_mid, direction_b_mid = directions(grad_mid, little[7])
-    direction_w_in, direction_b_in = directions(little[:6], little[6])
-    direction_w_out, direction_b_out = directions(little[8], little[9, :1])
-    return (
-        prices,
-        direction_w_in,
-        direction_b_in,
-        direction_w_mid,
-        direction_b_mid,
-        direction_w_out,
-        direction_b_out,
-    )
+    sums, sets = price_sums(params, increments)
+    prices, big, small = network(sets, sums, w_in, b_in, w_mid, b_mid, w_out, b_out)
+    return (prices, *finish(*sum_gradients(big, small)))
 
 
 def solution(mesh):

time: 175 us -> 140 us (0.80)
  the two profiles are of different devices: /device:TPU:1 before, /device:TPU:73 now
where the time goes in v2:
time: 140 us
  Pallas kernels  136 us (97%)
  local copies, waits for them, and re-layouts  2.67 us (2%)
    pallas_call x1, Pallas kernels, sum_gradients(): pl.pallas_call(sum_kernel, in_specs=[vmem, vmem], out_specs=[vmem, vmem],...  77 us
    pallas_call x1, Pallas kernels, price_sums(): pl.pallas_call(prices_kernel, grid=(BLOCKS,), in_specs=[pl.BlockSpec((8,...  41.7 us
    pallas_call x1, Pallas kernels, network(): pl.pallas_call(network_kernel, in_specs=[vmem] * 8 + [smem], out_specs=[v...  12.5 us
    pallas_call x1, Pallas kernels, finish(): pl.pallas_call(finish_kernel, in_specs=[vmem] * 2, out_specs=[vmem] * 6,...  4.89 us

profile of v2, /device:TPU:73, one launch (start us, length us, event | category | flops | bytes accessed | tf_op | source)
XLA Modules:
  0.0 140.0 jit_solution(4486716674160002716)
XLA Ops:
  1.3 1.3 reshape.40.w_out_ref
  2.6 1.4 pad.4.params_ref
  4.0 41.7 %prices.1 = (f32[8,128]{1,0:T(8,128)}, f32[8,128]{1,0:T(8,128)}) custom-call(f32[8,2048]{1,0:T(8,128)} %pad.4.params_ref, f32[8,128]{1,0:T(8,128)} %constant.7.clone.lag_ref, bf16[2,64,128]{2,1,0:T(8,128)(2,1)} %inc_ref.1), custom_call_target="tpu_custom_call" | custom-call | tf_op jit(solution)/shard_map/prices/pallas_call | solution.py:257
  45.6 12.5 %network.1 = (f32[8,88]{1,0:T(8,128)}, f32[1024,1024]{1,0:T(8,128)}, f32[16,1024]{1,0:T(8,128)}) custom-call(f32[8,128]{1,0:T(8,128)} %get-tuple-element.20.sets_ref, f32[88,128]{1,0:T(8,128)} %constant.8.clone.table_ref, f32[8,128]{1,0:T(8,128)} %get-tuple-element.21.prices_ref, bf16[6,1024]{1,0:T(8,128)(2,1)} %w_in_ref.1, f32[1,1024]{1,0:T(1,128)} %bitcast.10, ...), custom_call_target="tpu_custom_call" | custom-call | tf_op jit(solution)/shard_map/network/pallas_call | solution.py:561
  58.1 77.0 %gradients.1 = (f32[2,1024,512]{2,1,0:T(8,128)}, f32[2,16,512]{2,1,0:T(8,128)}) custom-call(f32[1024,1024]{1,0:T(8,128)} %get-tuple-element.23.big_ref, f32[16,1024]{1,0:T(8,128)} %get-tuple-element.24.small_ref), custom_call_target="tpu_custom_call" | custom-call | tf_op jit(solution)/shard_map/gradients/pallas_call | solution.py:440
  135.2 4.9 %finish.1 = (f32[6,1024]{1,0:T(8,128)}, f32[1,1024]{1,0:T(1,128)}, f32[1024,1024]{1,0:T(8,128)}, f32[1,1024]{1,0:T(1,128)}, f32[1,1024]{1,0:T(1,128)}, /*index=5*/f32[1,1]{1,0:T(1,128)}) custom-call(f32[2,1024,512]{2,1,0:T(8,128)} %get-tuple-element.25.big_ref, f32[2,16,512]{2,1,0:T(8,128)} %get-tuple-element.26.small_ref), custom_call_target="tpu_custom_call" | custom-call | tf_op jit(solution)/shard_map/finish/pallas_call | solution.py:622

commit v3 on v2

--- a/solution.py
+++ b/solution.py
@@ -133,7 +133,7 @@
             pl.semaphore_signal(barrier, inc=1, device_id=(peer,), device_id_type=MESH)
         for k in range(NX * NY):
             some = params_ref[:, pl.ds(k * 128, 128)]
-            some = jnp.concatenate([some, jnp.zeros((120, 128), jnp.float32)], axis=0).T
+            some = jnp.concatenate([some, jnp.zeros((124, 128), jnp.float32)], axis=0).T
             sets[k // NY, pl.ds((k % NY) * NZ, NZ)] = some.reshape(NZ, NC, OWN, 128)
         own_ref[...] = sets[x, y * NZ + z, core]
         noise[0] = inc_ref[0].astype(jnp.float32)
@@ -258,7 +258,7 @@
         prices_kernel,
         grid=(BLOCKS,),
         in_specs=[
-            pl.BlockSpec((8, BLOCKS * BLOCK), lambda b: (0, 0)),
+            pl.BlockSpec((4, BLOCKS * BLOCK), lambda b: (0, 0)),
             pl.BlockSpec((8, 128), lambda b: (0, 0)),
             pl.BlockSpec((2, STEPS, 128), lambda b: (0, 0, 0)),
         ],
@@ -286,7 +286,7 @@
         ],
         compiler_params=pltpu.CompilerParams(collective_id=0, has_side_effects=True),
         name="prices",
-    )(jnp.pad(params.T, ((0, 4), (0, 0))), jnp.asarray(lag_tables()), increments)
+    )(params.T, jnp.asarray(lag_tables()), increments)
 
 
 WIDE = 1024
@@ -298,176 +298,9 @@
 SLICE = HALF // NX
 
 
-def sum_kernel(
-    big_ref,
-    small_ref,
-    big_out,
-    small_out,
-    got_c,
-    half,
-    got_a,
-    mid,
-    got_b,
-    low,
-    got_z,
-    s_got_c,
-    s_got_a,
-    s_b,
-    s_z,
-    s_sum,
-    send_sem,
-    recv_sem,
-):
-    x, y, z, core = coords(lax.axis_index("paths"))
-    a = x * (1 - core) + y * core
-    b = y * (1 - core) + x * core
-
-    def at(aa, bb, zz):
-        return device_at(aa * (1 - core) + bb * core, bb * (1 - core) + aa * core, zz, core)
-
-    partner = device_at(x, y, z, 1 - core)
-    along_a = [at((a + d) % NX, b, z) for d in range(1, NX)]
-    along_b = [at(a, (b + d) % NY, z) for d in range(1, NY)]
-    along_z = [at(a, b, (z + d) % NZ) for d in range(1, NZ)]
-    peers = [partner] + along_a + along_b + along_z
-    barrier = pltpu.get_barrier_semaphore()
-    for peer in peers:
-        pl.semaphore_signal(barrier, inc=1, device_id=(peer,), device_id_type=MESH)
-    pl.semaphore_wait(barrier, len(peers))
-
-    count = [0]
-    started = []
-
-    def send(src, dst, peer):
-        k = count[0]
-        count[0] += 1
-        copy = pltpu.make_async_remote_copy(
-            src_ref=src,
-            dst_ref=dst,
-            send_sem=send_sem.at[k],
-            recv_sem=recv_sem.at[k],
-            device_id=(peer,),
-            device_id_type=MESH,
-        )
-        copy.start()
-        started.append(copy)
-        return copy
-
-    def part(index, size):
-        return pl.ds(pl.multiple_of(index * size, size), size)
-
-    own_cols, other_cols = part(core, HALF), part(1 - core, HALF)
-    big = send(big_ref.at[:, other_cols], got_c, partner)
-    little = send(small_ref.at[:, other_cols], s_got_c, partner)
-    little.wait_recv()
-    s_got_c[...] += small_ref[:, own_cols]
-    big.wait_recv()
-    half[...] = big_ref[:, own_cols] + got_c[...]
-
-    bigs, littles = [], []
-    for d in range(1, NX):
-        aa = (a + d) % NX
-        bigs.append(send(half.at[part(aa, ROWS_A), :], got_a.at[d - 1], along_a[d - 1]))
-        littles.append(send(s_got_c.at[:, part(aa, SLICE)], s_got_a.at[d - 1], along_a[d - 1]))
-    for d in range(1, NX):
-        littles[d - 1].wait_recv()
-    s_b[b] = s_got_c[:, part(a, SLICE)] + s_got_a[0] + s_got_a[1] + s_got_a[2]
-    for d in range(1, NX):
-        bigs[d - 1].wait_recv()
-    mid[...] = half[part(a, ROWS_A), :] + got_a[0] + got_a[1] + got_a[2]
-
-    bigs, littles = [], []
-    for d in range(1, NY):
-        bb = (b + d) % NY
-        bigs.append(send(mid.at[part(bb, ROWS_B), :], got_b.at[d - 1], along_b[d - 1]))
-        littles.append(send(s_b.at[b], s_b.at[b], along_b[d - 1]))
-    for d in range(1, NY):
-        littles[d - 1].wait_recv()
-    s_z[z] = (s_b[0] + s_b[1]) + (s_b[2] + s_b[3])
-    for d in range(1, NY):
-        bigs[d - 1].wait_recv()
-    low[...] = mid[part(b, ROWS_B), :] + got_b[0] + got_b[1] + got_b[2]
-
-    bigs, littles = [], []
-    for d in range(1, NZ):
-        zz = (z + d) % NZ
-        bigs.append(send(low.at[part(zz, ROWS_Z), :], got_z.at[d - 1], along_z[d - 1]))
-        littles.append(send(s_z.at[z], s_z.at[z], along_z[d - 1]))
-    for d in range(1, NZ):
-        littles[d - 1].wait_recv()
-    s_all = ((s_z[0] + s_z[1]) + (s_z[2] + s_z[3])) + ((s_z[4] + s_z[5]) + (s_z[6] + s_z[7]))
-    s_sum[:, part(a, SLICE)] = s_all
-    final = low[part(z, ROWS_Z), :]
-    for d in range(1, NZ):
-        bigs[d - 1].wait_recv()
-        final = final + got_z[d - 1]
-
-    base_b = a * ROWS_A + b * ROWS_B
-    mine = pl.ds(pl.multiple_of(base_b + z * ROWS_Z, ROWS_Z), ROWS_Z)
-    half_out = big_out.at[core]
-    half_out[mine, :] = final
-    bigs = [send(half_out.at[mine, :], half_out.at[mine, :], peer) for peer in along_z]
-    littles = [
-        send(s_sum.at[:, part(a, SLICE)], s_sum.at[:, part(a, SLICE)], peer) for peer in along_a
-    ]
-    for copy in bigs:
-        copy.wait_recv()
-    rows_b = pl.ds(pl.multiple_of(base_b, ROWS_B), ROWS_B)
-    bigs = [send(half_out.at[rows_b, :], half_out.at[rows_b, :], peer) for peer in along_b]
-    for copy in littles:
-        copy.wait_recv()
-    small_out[core] = s_sum[...]
-    little = send(small_out.at[core], small_out.at[core], partner)
-    for copy in bigs:
-        copy.wait_recv()
-    rows_a = part(a, ROWS_A)
-    bigs = [send(half_out.at[rows_a, :], half_out.at[rows_a, :], peer) for peer in along_a]
-    for copy in bigs:
-        copy.wait_recv()
-    big = send(half_out, half_out, partner)
-    little.wait_recv()
-    big.wait_recv()
-    for copy in started:
-        copy.wait_send()
-
-
-SENDS = 2 + 2 * (NX - 1) + 2 * (NY - 1) + 2 * (NZ - 1) + (NZ - 1) + (NX - 1) + (NY - 1) + (NX - 1) + 2
-
-
-def sum_gradients(big, small):
-    f32 = jnp.float32
-    vmem = pl.BlockSpec(memory_space=pltpu.VMEM)
-    return pl.pallas_call(
-        sum_kernel,
-        in_specs=[vmem, vmem],
-        out_specs=[vmem, vmem],
-        out_shape=[
-            jax.ShapeDtypeStruct((NC, WIDE, HALF), f32),
-            jax.ShapeDtypeStruct((NC, SMALL, HALF), f32),
-        ],
-        scratch_shapes=[
-            pltpu.VMEM((WIDE, HALF), f32),
-            pltpu.VMEM((WIDE, HALF), f32),
-            pltpu.VMEM((NX - 1, ROWS_A, HALF), f32),
-            pltpu.VMEM((ROWS_A, HALF), f32),
-            pltpu.VMEM((NY - 1, ROWS_B, HALF), f32),
-            pltpu.VMEM((ROWS_B, HALF), f32),
-            pltpu.VMEM((NZ - 1, ROWS_Z, HALF), f32),
-            pltpu.VMEM((SMALL, HALF), f32),
-            pltpu.VMEM((NX - 1, SMALL, SLICE), f32),
-            pltpu.VMEM((NY, SMALL, SLICE), f32),
-            pltpu.VMEM((NZ, SMALL, SLICE), f32),
-            pltpu.VMEM((SMALL, HALF), f32),
-            pltpu.SemaphoreType.DMA((SENDS,)),
-            pltpu.SemaphoreType.DMA((SENDS,)),
-        ],
-        compiler_params=pltpu.CompilerParams(collective_id=1, has_side_effects=True),
-        name="gradients",
-    )(big, small)
-
-
 ROWS = PAIRS * OWN
 CHUNK = ROWS // 4
+DEPTH = 768
 
 
 def pair_table():
@@ -481,7 +314,7 @@
     return table
 
 
-def network_kernel(
+def network_part(
     sets_ref,
     table_ref,
     prices_ref,
@@ -492,13 +325,13 @@
     w_out_ref,
     b_out_ref,
     prices_out,
-    big_ref,
     small_ref,
     feats,
     hid_in,
     slope_in,
     delta_mid,
     delta_in,
+    hid_turn,
 ):
     f32, bf16 = jnp.float32, jnp.bfloat16
     pairs = CHUNK // OWN
@@ -512,6 +345,8 @@
     g_bmid = jnp.zeros((8, WIDE), f32)
     g_bin = jnp.zeros((8, WIDE), f32)
     g_bout = jnp.zeros((8, 1), f32)
+    hid_in[pl.ds(ROWS, DEPTH - ROWS), :] = jnp.zeros((DEPTH - ROWS, WIDE), bf16)
+    delta_mid[pl.ds(ROWS, DEPTH - ROWS), :] = jnp.zeros((DEPTH - ROWS, WIDE), bf16)
     for c in range(ROWS // CHUNK):
         rows = pl.ds(c * CHUNK, CHUNK)
         table = table_ref[pl.ds(c * pairs, pairs), :]
@@ -549,36 +384,248 @@
     small_ref[pl.ds(8, 1), :] = jnp.sum(g_out, axis=0, keepdims=True)
     small_ref[pl.ds(9, 1), :] = jnp.broadcast_to(jnp.sum(g_bout, axis=0, keepdims=True), (1, WIDE))
     small_ref[pl.ds(10, 6), :] = jnp.zeros((6, WIDE), f32)
-    big_ref[...] = lax.dot_general(
-        hid_in[...], delta_mid[...], (((0,), (0,)), ((), ())), preferred_element_type=f32
+    hid_turn[...] = hid_in[...].T
+
+
+LATER = (1, 2, 3, 0)
+SENDS = 84
+
+
+def train_kernel(
+    sets_ref,
+    table_ref,
+    prices_ref,
+    w_in_ref,
+    b_in_ref,
+    w_mid_ref,
+    b_mid_ref,
+    w_out_ref,
+    b_out_ref,
+    prices_out,
+    big_out,
+    small_out,
+    small,
+    feats,
+    hid_in,
+    slope_in,
+    delta_mid,
+    delta_in,
+    hid_turn,
+    other,
+    got_c,
+    work,
+    got_a,
+    mid,
+    got_b,
+    low,
+    got_z,
+    s_got_c,
+    s_got_a,
+    s_b,
+    s_z,
+    s_sum,
+    send_sem,
+    recv_sem,
+):
+    x, y, z, core = coords(lax.axis_index("paths"))
+    a = x * (1 - core) + y * core
+    b = y * (1 - core) + x * core
+
+    def at(aa, bb, zz):
+        return device_at(aa * (1 - core) + bb * core, bb * (1 - core) + aa * core, zz, core)
+
+    partner = device_at(x, y, z, 1 - core)
+    along_a = [at((a + d) % NX, b, z) for d in range(1, NX)]
+    along_b = [at(a, (b + d) % NY, z) for d in range(1, NY)]
+    along_z = [at(a, b, (z + d) % NZ) for d in range(1, NZ)]
+    peers = [partner] + along_a + along_b + along_z
+    barrier = pltpu.get_barrier_semaphore()
+    for peer in peers:
+        pl.semaphore_signal(barrier, inc=1, device_id=(peer,), device_id_type=MESH)
+
+    network_part(
+        sets_ref,
+        table_ref,
+        prices_ref,
+        w_in_ref,
+        b_in_ref,
+        w_mid_ref,
+        b_mid_ref,
+        w_out_ref,
+        b_out_ref,
+        prices_out,
+        small,
+        feats,
+        hid_in,
+        slope_in,
+        delta_mid,
+        delta_in,
+        hid_turn,
     )
-
-
-def network(sets, prices, w_in, b_in, w_mid, b_mid, w_out, b_out):
+    pl.semaphore_wait(barrier, len(peers))
+
+    count = [0]
+    started = []
+
+    def send(src, dst, peer):
+        k = count[0]
+        count[0] += 1
+        copy = pltpu.make_async_remote_copy(
+            src_ref=src,
+            dst_ref=dst,
+            send_sem=send_sem.at[k],
+            recv_sem=recv_sem.at[k],
+            device_id=(peer,),
+            device_id_type=MESH,
+        )
+        copy.start()
+        started.append(copy)
+        return copy
+
+    def part(index, size):
+        return pl.ds(pl.multiple_of(index * size, size), size)
+
+    def rows_of(aa, bb):
+        return part((aa % NX) * NY + bb % NY, ROWS_B)
+
+    def product(first, second, e, cols):
+        left = jnp.concatenate(
+            [hid_turn[rows_of(first + d, second + e), :] for d in range(NX)], axis=0
+        )
+        out = jnp.dot(left, delta_mid[:, cols], preferred_element_type=jnp.float32)
+        return out.reshape(NX, ROWS_B, HALF)
+
+    own_cols, other_cols = part(core, HALF), part(1 - core, HALF)
+    little = send(small.at[:, other_cols], s_got_c, partner)
+    pair = {}
+    for e in LATER:
+        other[e] = product(b, a, e, other_cols)
+        pair[e] = send(other.at[e], got_c.at[e], partner)
+    little.wait_recv()
+    s_got_c[...] += small[:, own_cols]
+    littles = []
+    for d in range(1, NX):
+        littles.append(
+            send(s_got_c.at[:, part((a + d) % NX, SLICE)], s_got_a.at[d - 1], along_a[d - 1])
+        )
+    steps = {}
+    for e in LATER:
+        mine = product(a, b, e, own_cols)
+        pair[e].wait_recv()
+        work[e] = mine + got_c[e]
+        steps[e] = [
+            send(work.at[e, d], got_a.at[e, d - 1], along_a[d - 1]) for d in range(1, NX)
+        ]
+    for copy in littles:
+        copy.wait_recv()
+    s_b[b] = s_got_c[:, part(a, SLICE)] + s_got_a[0] + s_got_a[1] + s_got_a[2]
+    littles = [send(s_b.at[b], s_b.at[b], peer) for peer in along_b]
+    across = []
+    for e in LATER:
+        for copy in steps[e]:
+            copy.wait_recv()
+        mid[e] = work[e, 0] + got_a[e, 0] + got_a[e, 1] + got_a[e, 2]
+        if e > 0:
+            across.append(send(mid.at[e], got_b.at[e - 1], along_b[e - 1]))
+    for copy in littles:
+        copy.wait_recv()
+    s_z[z] = (s_b[0] + s_b[1]) + (s_b[2] + s_b[3])
+    littles = [send(s_z.at[z], s_z.at[z], peer) for peer in along_z]
+    for copy in across:
+        copy.wait_recv()
+    low[...] = mid[0] + got_b[0] + got_b[1] + got_b[2]
+    deep = [
+        send(low.at[part((z + d) % NZ, ROWS_Z), :], got_z.at[d - 1], along_z[d - 1])
+        for d in range(1, NZ)
+    ]
+    for copy in littles:
+        copy.wait_recv()
+    s_all = ((s_z[0] + s_z[1]) + (s_z[2] + s_z[3])) + ((s_z[4] + s_z[5]) + (s_z[6] + s_z[7]))
+    s_sum[:, part(a, SLICE)] = s_all
+    littles = [
+        send(s_sum.at[:, part(a, SLICE)], s_sum.at[:, part(a, SLICE)], peer) for peer in along_a
+    ]
+    final = low[part(z, ROWS_Z), :]
+    for d in range(1, NZ):
+        deep[d - 1].wait_recv()
+        final = final + got_z[d - 1]
+
+    half_out = big_out.at[core]
+    mine = part((a * NY + b) * NZ + z, ROWS_Z)
+    half_out[mine, :] = final
+    deep = [send(half_out.at[mine, :], half_out.at[mine, :], peer) for peer in along_z]
+    for copy in littles:
+        copy.wait_recv()
+    small_out[core] = s_sum[...]
+    little = send(small_out.at[core], small_out.at[core], partner)
+    for copy in deep:
+        copy.wait_recv()
+
+    def spread(rows, targets):
+        return [send(half_out.at[rows, :], half_out.at[rows, :], peer) for peer in targets]
+
+    across = spread(rows_of(a, b), along_b)
+    steps = [spread(rows_of(a, b), along_a)]
+    pairs = spread(rows_of(a, b), [partner])
+    for d in range(1, NY):
+        across[d - 1].wait_recv()
+        rows = rows_of(a, b + NY - d)
+        steps.append(spread(rows, along_a))
+        pairs += spread(rows, [partner])
+    for e in range(NY):
+        for d in range(1, NX):
+            steps[e][d - 1].wait_recv()
+            pairs += spread(rows_of(a + NX - d, b + NY - e), [partner])
+    little.wait_recv()
+    for copy in pairs:
+        copy.wait_recv()
+    for copy in started:
+        copy.wait_send()
+
+
+def train(sets, sums, w_in, b_in, w_mid, b_mid, w_out, b_out):
     f32, bf16 = jnp.float32, jnp.bfloat16
     vmem = pl.BlockSpec(memory_space=pltpu.VMEM)
     smem = pl.BlockSpec(memory_space=pltpu.SMEM)
     return pl.pallas_call(
-        network_kernel,
+        train_kernel,
         in_specs=[vmem] * 8 + [smem],
         out_specs=[vmem, vmem, vmem],
         out_shape=[
             jax.ShapeDtypeStruct((OWN, PAIRS), f32),
-            jax.ShapeDtypeStruct((WIDE, WIDE), f32),
-            jax.ShapeDtypeStruct((SMALL, WIDE), f32),
+            jax.ShapeDtypeStruct((NC, WIDE, HALF), f32),
+            jax.ShapeDtypeStruct((NC, SMALL, HALF), f32),
         ],
         scratch_shapes=[
+            pltpu.VMEM((SMALL, WIDE), f32),
             pltpu.VMEM((ROWS, 128), bf16),
+            pltpu.VMEM((DEPTH, WIDE), bf16),
+            pltpu.VMEM((ROWS, WIDE), f32),
+            pltpu.VMEM((DEPTH, WIDE), bf16),
             pltpu.VMEM((ROWS, WIDE), bf16),
-            pltpu.VMEM((ROWS, WIDE), f32),
-            pltpu.VMEM((ROWS, WIDE), bf16),
-            pltpu.VMEM((ROWS, WIDE), bf16),
+            pltpu.VMEM((WIDE, DEPTH), bf16),
+            pltpu.VMEM((NY, NX, ROWS_B, HALF), f32),
+            pltpu.VMEM((NY, NX, ROWS_B, HALF), f32),
+            pltpu.VMEM((NY, NX, ROWS_B, HALF), f32),
+            pltpu.VMEM((NY, NX - 1, ROWS_B, HALF), f32),
+            pltpu.VMEM((NY, ROWS_B, HALF), f32),
+            pltpu.VMEM((NY - 1, ROWS_B, HALF), f32),
+            pltpu.VMEM((ROWS_B, HALF), f32),
+            pltpu.VMEM((NZ - 1, ROWS_Z, HALF), f32),
+            pltpu.VMEM((SMALL, HALF), f32),
+            pltpu.VMEM((NX - 1, SMALL, SLICE), f32),
+            pltpu.VMEM((NY, SMALL, SLICE), f32),
+            pltpu.VMEM((NZ, SMALL, SLICE), f32),
+            pltpu.VMEM((SMALL, HALF), f32),
+            pltpu.SemaphoreType.DMA((SENDS,)),
+            pltpu.SemaphoreType.DMA((SENDS,)),
         ],
-        name="network",
+        compiler_params=pltpu.CompilerParams(collective_id=1, has_side_effects=True),
+        name="train",
     )(
         sets,
         jnp.asarray(pair_table()),
-        prices,
+        sums,
         w_in,
         b_in.reshape(1, WIDE),
         w_mid,
@@ -631,8 +678,8 @@
 
 def on_device(params, increments, w_in, b_in, w_mid, b_mid, w_out, b_out):
     sums, sets = price_sums(params, increments)
-    prices, big, small = network(sets, sums, w_in, b_in, w_mid, b_mid, w_out, b_out)
-    return (prices, *finish(*sum_gradients(big, small)))
+    prices, big, small = train(sets, sums, w_in, b_in, w_mid, b_mid, w_out, b_out)
+    return (prices, *finish(big, small))
 
 
 def solution(mesh):

time: 140 us -> 122 us (0.87)
  the two profiles are of different devices: /device:TPU:73 before, /device:TPU:1 now
where the time goes in v3:
time: 122 us; the launch traced here: 121 us
  Pallas kernels  118 us (97%)
  local copies, waits for them, and re-layouts  1.88 us (2%)
  between operations  1.31 us (1%)
    pallas_call x1, Pallas kernels, train(): pl.pallas_call(train_kernel, in_specs=[vmem] * 8 + [smem], out_specs=[vme...  67.5 us
    pallas_call x1, Pallas kernels, price_sums(): pl.pallas_call(prices_kernel, grid=(BLOCKS,), in_specs=[pl.BlockSpec((4,...  45.8 us
    pallas_call x1, Pallas kernels, finish(): pl.pallas_call(finish_kernel, in_specs=[vmem] * 2, out_specs=[vmem] * 6,...  4.89 us

profile of v3, /device:TPU:1, one launch (start us, length us, event | category | flops | bytes accessed | tf_op | source)
XLA Modules:
  0.0 121.4 jit_solution(11479525515266342946)
XLA Ops:
  1.3 1.3 %reshape.40.w_out_ref = bf16[1,1024]{1,0:T(2,128)(2,1)} reshape(bf16[1024]{0:T(1024)(128)(2,1)} %param.16) | data formatting | bytes 4096 | tf_op jit(solution)/shard_map/reshape | solution.py:633
  2.6 45.8 %prices.1 = (f32[8,128]{1,0:T(8,128)}, f32[8,128]{1,0:T(8,128)}) custom-call(f32[4,2048]{1,0:T(4,128)} %bitcast.9, f32[8,128]{1,0:T(8,128)} %constant.4.clone.lag_ref, bf16[2,64,128]{2,1,0:T(8,128)(2,1)} %inc_ref.1), custom_call_target="tpu_custom_call" | custom-call | tf_op jit(solution)/shard_map/prices/pallas_call | solution.py:257
  48.4 67.5 %train.1 = (f32[8,88]{1,0:T(8,128)}, f32[2,1024,512]{2,1,0:T(8,128)}, f32[2,16,512]{2,1,0:T(8,128)}) custom-call(f32[8,128]{1,0:T(8,128)} %get-tuple-element.18.sets_ref, f32[88,128]{1,0:T(8,128)} %constant.5.clone.table_ref, f32[8,128]{1,0:T(8,128)} %get-tuple-element.19.prices_ref, bf16[6,1024]{1,0:T(8,128)(2,1)} %w_in_ref.1, f32[1,1024]{1,0:T(1,128)} %bitcast.10, ...), custom_call_target="tpu_custom_call" | custom-call | tf_op jit(solution)/shard_map/train/pallas_call | solution.py:590
  115.9 0.0 copy-start
  115.9 4.9 %finish.1 = (f32[6,1024]{1,0:T(8,128)}, f32[1,1024]{1,0:T(1,128)}, f32[1024,1024]{1,0:T(8,128)}, f32[1,1024]{1,0:T(1,128)}, f32[1,1024]{1,0:T(1,128)}, /*index=5*/f32[1,1]{1,0:T(1,128)}) custom-call(f32[2,1024,512]{2,1,0:T(8,128)} %get-tuple-element.21.big_ref, f32[2,16,512]{2,1,0:T(8,128)} %get-tuple-element.22.small_ref), custom_call_target="tpu_custom_call" | custom-call | tf_op jit(solution)/shard_map/finish/pallas_call | solution.py:669
  120.8 0.0 copy-done
  120.8 0.6 copy.19
Async XLA Ops:
  115.9 4.9 %copy-start = (f32[8,88]{1,0:T(8,128)S(1)}, f32[8,88]{1,0:T(8,128)}, u32[]{:S(2)}) copy-start(f32[8,88]{1,0:T(8,128)} %get-tuple-element.36) | copy-start | bytes 8452

commit v4 on v3

--- a/solution.py
+++ b/solution.py
@@ -388,7 +388,9 @@
 
 
 LATER = (1, 2, 3, 0)
-SENDS = 84
+PARTS = 2
+COLS = HALF // PARTS
+SENDS = 64 * PARTS + 18
 
 
 def train_kernel(
@@ -404,6 +406,8 @@
     prices_out,
     big_out,
     small_out,
+    square_out,
+    big,
     small,
     feats,
     hid_in,
@@ -426,6 +430,7 @@
     s_sum,
     send_sem,
     recv_sem,
+    out_sem,
 ):
     x, y, z, core = coords(lax.axis_index("paths"))
     a = x * (1 - core) + y * core
@@ -488,56 +493,116 @@
     def rows_of(aa, bb):
         return part((aa % NX) * NY + bb % NY, ROWS_B)
 
-    def product(first, second, e, cols):
+    def product(first, second, e, column):
         left = jnp.concatenate(
             [hid_turn[rows_of(first + d, second + e), :] for d in range(NX)], axis=0
         )
-        out = jnp.dot(left, delta_mid[:, cols], preferred_element_type=jnp.float32)
-        return out.reshape(NX, ROWS_B, HALF)
-
+        right = delta_mid[:, part(column, COLS)]
+        out = jnp.dot(left, right, preferred_element_type=jnp.float32)
+        return out.reshape(NX, ROWS_B, COLS)
+
+    mine = part((a * NY + b) * NZ + z, ROWS_Z)
     own_cols, other_cols = part(core, HALF), part(1 - core, HALF)
+    pair, steps, across, deep, pairs = {}, {}, {}, {}, {}
+
+    def to_partner(h):
+        for e in LATER:
+            other[h, e] = product(b, a, e, (1 - core) * PARTS + h)
+            pair[h, e] = send(other.at[h, e], got_c.at[h, e], partner)
+
+    def along_first(h):
+        for e in LATER:
+            value = product(a, b, e, core * PARTS + h)
+            pair[h, e].wait_recv()
+            work[h, e] = value + got_c[h, e]
+            steps[h, e] = [
+                send(work.at[h, e, d], got_a.at[h, e, d - 1], along_a[d - 1])
+                for d in range(1, NX)
+            ]
+
+    def along_second(h):
+        across[h] = []
+        for e in LATER:
+            for copy in steps[h, e]:
+                copy.wait_recv()
+            mid[h, e] = work[h, e, 0] + got_a[h, e, 0] + got_a[h, e, 1] + got_a[h, e, 2]
+            if e > 0:
+                across[h].append(send(mid.at[h, e], got_b.at[h, e - 1], along_b[e - 1]))
+
+    def along_third(h):
+        for copy in across[h]:
+            copy.wait_recv()
+        low[h] = mid[h, 0] + got_b[h, 0] + got_b[h, 1] + got_b[h, 2]
+        deep[h] = [
+            send(low.at[h, part((z + d) % NZ, ROWS_Z), :], got_z.at[h, d - 1], along_z[d - 1])
+            for d in range(1, NZ)
+        ]
+
+    def spread(h, rows, targets):
+        half = big.at[core, h]
+        return [send(half.at[rows, :], half.at[rows, :], peer) for peer in targets]
+
+    def gather_third(h):
+        final = low[h, part(z, ROWS_Z), :]
+        for d in range(1, NZ):
+            deep[h][d - 1].wait_recv()
+            final = final + got_z[h, d - 1]
+        big[core, h, mine, :] = final
+        deep[h] = spread(h, mine, along_z)
+
+    def gather_second(h):
+        for copy in deep[h]:
+            copy.wait_recv()
+        rows = rows_of(a, b)
+        across[h] = spread(h, rows, along_b)
+        steps[h] = [spread(h, rows, along_a)]
+        pairs[h] = spread(h, rows, [partner])
+
+    def gather_first(h):
+        for d in range(1, NY):
+            across[h][d - 1].wait_recv()
+            rows = rows_of(a, b + NY - d)
+            steps[h].append(spread(h, rows, along_a))
+            pairs[h] += spread(h, rows, [partner])
+
+    def share(h):
+        for e in range(NY):
+            for d in range(1, NX):
+                steps[h][e][d - 1].wait_recv()
+                pairs[h] += spread(h, rows_of(a + NX - d, b + NY - e), [partner])
+
+    def store(h, c):
+        copy = pltpu.make_async_copy(big.at[c, h], big_out.at[c, h], out_sem.at[h, c])
+        copy.start()
+        total = jnp.zeros((8, COLS), jnp.float32)
+        for k in range(8):
+            block = big[c, h, pl.ds(k * 128, 128), :].reshape(16, 8, COLS)
+            total = total + jnp.sum(block * block, axis=0)
+        return copy, total
+
     little = send(small.at[:, other_cols], s_got_c, partner)
-    pair = {}
-    for e in LATER:
-        other[e] = product(b, a, e, other_cols)
-        pair[e] = send(other.at[e], got_c.at[e], partner)
+    to_partner(0)
+    to_partner(1)
     little.wait_recv()
     s_got_c[...] += small[:, own_cols]
-    littles = []
-    for d in range(1, NX):
-        littles.append(
-            send(s_got_c.at[:, part((a + d) % NX, SLICE)], s_got_a.at[d - 1], along_a[d - 1])
-        )
-    steps = {}
-    for e in LATER:
-        mine = product(a, b, e, own_cols)
-        pair[e].wait_recv()
-        work[e] = mine + got_c[e]
-        steps[e] = [
-            send(work.at[e, d], got_a.at[e, d - 1], along_a[d - 1]) for d in range(1, NX)
-        ]
+    littles = [
+        send(s_got_c.at[:, part((a + d) % NX, SLICE)], s_got_a.at[d - 1], along_a[d - 1])
+        for d in range(1, NX)
+    ]
+    along_first(0)
+    along_first(1)
     for copy in littles:
         copy.wait_recv()
     s_b[b] = s_got_c[:, part(a, SLICE)] + s_got_a[0] + s_got_a[1] + s_got_a[2]
     littles = [send(s_b.at[b], s_b.at[b], peer) for peer in along_b]
-    across = []
-    for e in LATER:
-        for copy in steps[e]:
-            copy.wait_recv()
-        mid[e] = work[e, 0] + got_a[e, 0] + got_a[e, 1] + got_a[e, 2]
-        if e > 0:
-            across.append(send(mid.at[e], got_b.at[e - 1], along_b[e - 1]))
+    along_second(0)
     for copy in littles:
         copy.wait_recv()
     s_z[z] = (s_b[0] + s_b[1]) + (s_b[2] + s_b[3])
     littles = [send(s_z.at[z], s_z.at[z], peer) for peer in along_z]
-    for copy in across:
-        copy.wait_recv()
-    low[...] = mid[0] + got_b[0] + got_b[1] + got_b[2]
-    deep = [
-        send(low.at[part((z + d) % NZ, ROWS_Z), :], got_z.at[d - 1], along_z[d - 1])
-        for d in range(1, NZ)
-    ]
+    along_third(0)
+    gather_third(0)
+    along_second(1)
     for copy in littles:
         copy.wait_recv()
     s_all = ((s_z[0] + s_z[1]) + (s_z[2] + s_z[3])) + ((s_z[4] + s_z[5]) + (s_z[6] + s_z[7]))
@@ -545,40 +610,36 @@
     littles = [
         send(s_sum.at[:, part(a, SLICE)], s_sum.at[:, part(a, SLICE)], peer) for peer in along_a
     ]
-    final = low[part(z, ROWS_Z), :]
-    for d in range(1, NZ):
-        deep[d - 1].wait_recv()
-        final = final + got_z[d - 1]
-
-    half_out = big_out.at[core]
-    mine = part((a * NY + b) * NZ + z, ROWS_Z)
-    half_out[mine, :] = final
-    deep = [send(half_out.at[mine, :], half_out.at[mine, :], peer) for peer in along_z]
+    gather_second(0)
+    along_third(1)
+    gather_first(0)
     for copy in littles:
         copy.wait_recv()
     small_out[core] = s_sum[...]
     little = send(small_out.at[core], small_out.at[core], partner)
-    for copy in deep:
+    gather_third(1)
+    share(0)
+    gather_second(1)
+    gather_first(1)
+    stores = [store(0, core)]
+    for copy in pairs[0]:
         copy.wait_recv()
-
-    def spread(rows, targets):
-        return [send(half_out.at[rows, :], half_out.at[rows, :], peer) for peer in targets]
-
-    across = spread(rows_of(a, b), along_b)
-    steps = [spread(rows_of(a, b), along_a)]
-    pairs = spread(rows_of(a, b), [partner])
-    for d in range(1, NY):
-        across[d - 1].wait_recv()
-        rows = rows_of(a, b + NY - d)
-        steps.append(spread(rows, along_a))
-        pairs += spread(rows, [partner])
-    for e in range(NY):
-        for d in range(1, NX):
-            steps[e][d - 1].wait_recv()
-            pairs += spread(rows_of(a + NX - d, b + NY - e), [partner])
+    stores.append(store(0, 1 - core))
+    share(1)
+    stores.append(store(1, core))
     little.wait_recv()
-    for copy in pairs:
+    for copy in pairs[1]:
         copy.wait_recv()
+    stores.append(store(1, 1 - core))
+    squares = [total for copy, total in stores]
+    own_squares = squares[0] + squares[2]
+    other_squares = squares[1] + squares[3]
+    first = own_squares * (1 - core).astype(jnp.float32) + other_squares * core.astype(jnp.float32)
+    second = own_squares * core.astype(jnp.float32) + other_squares * (1 - core).astype(jnp.float32)
+    square_out[0] = first
+    square_out[1] = second
+    for copy, total in stores:
+        copy.wait()
     for copy in started:
         copy.wait_send()
 
@@ -590,13 +651,15 @@
     return pl.pallas_call(
         train_kernel,
         in_specs=[vmem] * 8 + [smem],
-        out_specs=[vmem, vmem, vmem],
+        out_specs=[vmem, pl.BlockSpec(memory_space=pl.ANY), vmem, vmem],
         out_shape=[
             jax.ShapeDtypeStruct((OWN, PAIRS), f32),
-            jax.ShapeDtypeStruct((NC, WIDE, HALF), f32),
+            jax.ShapeDtypeStruct((NC, PARTS, WIDE, COLS), f32),
             jax.ShapeDtypeStruct((NC, SMALL, HALF), f32),
+            jax.ShapeDtypeStruct((NC, 8, COLS), f32),
         ],
         scratch_shapes=[
+            pltpu.VMEM((NC, PARTS, WIDE, COLS), f32),
             pltpu.VMEM((SMALL, WIDE), f32),
             pltpu.VMEM((ROWS, 128), bf16),
             pltpu.VMEM((DEPTH, WIDE), bf16),
@@ -604,14 +667,14 @@
             pltpu.VMEM((DEPTH, WIDE), bf16),
             pltpu.VMEM((ROWS, WIDE), bf16),
             pltpu.VMEM((WIDE, DEPTH), bf16),
-            pltpu.VMEM((NY, NX, ROWS_B, HALF), f32),
-            pltpu.VMEM((NY, NX, ROWS_B, HALF), f32),
-            pltpu.VMEM((NY, NX, ROWS_B, HALF), f32),
-            pltpu.VMEM((NY, NX - 1, ROWS_B, HALF), f32),
-            pltpu.VMEM((NY, ROWS_B, HALF), f32),
-            pltpu.VMEM((NY - 1, ROWS_B, HALF), f32),
-            pltpu.VMEM((ROWS_B, HALF), f32),
-            pltpu.VMEM((NZ - 1, ROWS_Z, HALF), f32),
+            pltpu.VMEM((PARTS, NY, NX, ROWS_B, COLS), f32),
+            pltpu.VMEM((PARTS, NY, NX, ROWS_B, COLS), f32),
+            pltpu.VMEM((PARTS, NY, NX, ROWS_B, COLS), f32),
+            pltpu.VMEM((PARTS, NY, NX - 1, ROWS_B, COLS), f32),
+            pltpu.VMEM((PARTS, NY, ROWS_B, COLS), f32),
+            pltpu.VMEM((PARTS, NY - 1, ROWS_B, COLS), f32),
+            pltpu.VMEM((PARTS, ROWS_B, COLS), f32),
+            pltpu.VMEM((PARTS, NZ - 1, ROWS_Z, COLS), f32),
             pltpu.VMEM((SMALL, HALF), f32),
             pltpu.VMEM((NX - 1, SMALL, SLICE), f32),
             pltpu.VMEM((NY, SMALL, SLICE), f32),
@@ -619,6 +682,7 @@
             pltpu.VMEM((SMALL, HALF), f32),
             pltpu.SemaphoreType.DMA((SENDS,)),
             pltpu.SemaphoreType.DMA((SENDS,)),
+            pltpu.SemaphoreType.DMA((PARTS, NC)),
         ],
         compiler_params=pltpu.CompilerParams(collective_id=1, has_side_effects=True),
         name="train",
@@ -635,51 +699,65 @@
     )
 
 
+TILES = 4
+TILE = WIDE // TILES
+
+
 def finish_kernel(
-    big_ref, small_ref, w_in_out, b_in_out, w_mid_out, b_mid_out, w_out_out, b_out_out
+    big_ref, small_ref, square_ref, w_in_out, b_in_out, w_mid_out, b_mid_out, w_out_out, b_out_out
 ):
     def factor(total, entries):
         return lax.rsqrt(total * (1.0 / entries) + EPSILON)
 
+    def total(value):
+        return jnp.sum(jnp.sum(value, axis=1, keepdims=True), axis=0, keepdims=True)
+
     def sumsq(value):
-        return jnp.sum(jnp.sum(value * value, axis=1, keepdims=True), axis=0, keepdims=True)
-
-    small = jnp.concatenate([small_ref[0], small_ref[1]], axis=1)
-    g_bout = small[9:10, 0:1]
-    s_mid = sumsq(small[7:8])
-    for k in range(8):
-        for c in range(NC):
-            s_mid = s_mid + sumsq(big_ref[c, pl.ds(k * 128, 128), :])
-    f_in = factor(sumsq(small[0:7]), 7 * WIDE)
-    f_mid = factor(s_mid, (WIDE + 1) * WIDE)
-    f_out = factor(sumsq(small[8:9]) + g_bout * g_bout, WIDE + 1)
-    w_in_out[...] = small[0:6] * f_in
-    b_in_out[...] = small[6:7] * f_in
-    b_mid_out[...] = small[7:8] * f_mid
-    w_out_out[...] = small[8:9] * f_out
-    b_out_out[...] = g_bout * f_out
+        return total(value * value)
+
+    bias = sumsq(small_ref[0, 7:8, :]) + sumsq(small_ref[1, 7:8, :])
+    f_mid = factor(total(square_ref[0] + square_ref[1]) + bias, (WIDE + 1) * WIDE)
     for c in range(NC):
-        w_mid_out[:, pl.ds(c * HALF, HALF)] = big_ref[c] * f_mid
-
-
-def finish(big, small):
+        for h in range(PARTS):
+            w_mid_out[:, pl.ds((c * PARTS + h) * COLS, COLS)] = big_ref[c, h] * f_mid
+
+    @pl.when(pl.program_id(0) == 0)
+    def _():
+        small = jnp.concatenate([small_ref[0], small_ref[1]], axis=1)
+        g_bout = small[9:10, 0:1]
+        f_in = factor(sumsq(small[0:7]), 7 * WIDE)
+        f_out = factor(sumsq(small[8:9]) + g_bout * g_bout, WIDE + 1)
+        w_in_out[...] = small[0:6] * f_in
+        b_in_out[...] = small[6:7] * f_in
+        b_mid_out[...] = small[7:8] * f_mid
+        w_out_out[...] = small[8:9] * f_out
+        b_out_out[...] = g_bout * f_out
+
+
+def finish(big, small, squares):
     f32 = jnp.float32
-    vmem = pl.BlockSpec(memory_space=pltpu.VMEM)
     shapes = [(6, WIDE), (1, WIDE), (WIDE, WIDE), (1, WIDE), (1, WIDE), (1, 1)]
+    blocks = [(6, WIDE), (1, WIDE), (TILE, WIDE), (1, WIDE), (1, WIDE), (1, 1)]
+    moves = [lambda i: (0, 0)] * 2 + [lambda i: (i, 0)] + [lambda i: (0, 0)] * 3
     w_in, b_in, w_mid, b_mid, w_out, b_out = pl.pallas_call(
         finish_kernel,
-        in_specs=[vmem] * 2,
-        out_specs=[vmem] * 6,
+        grid=(TILES,),
+        in_specs=[
+            pl.BlockSpec((NC, PARTS, TILE, COLS), lambda i: (0, 0, i, 0)),
+            pl.BlockSpec((NC, SMALL, HALF), lambda i: (0, 0, 0)),
+            pl.BlockSpec((NC, 8, COLS), lambda i: (0, 0, 0)),
+        ],
+        out_specs=[pl.BlockSpec(block, move) for block, move in zip(blocks, moves)],
         out_shape=[jax.ShapeDtypeStruct(shape, f32) for shape in shapes],
         name="finish",
-    )(big, small)
+    )(big, small, squares)
     return w_in, b_in.reshape(WIDE), w_mid, b_mid.reshape(WIDE), w_out.reshape(WIDE), b_out.reshape(1)
 
 
 def on_device(params, increments, w_in, b_in, w_mid, b_mid, w_out, b_out):
     sums, sets = price_sums(params, increments)
-    prices, big, small = train(sets, sums, w_in, b_in, w_mid, b_mid, w_out, b_out)
-    return (prices, *finish(big, small))
+    prices, big, small, squares = train(sets, sums, w_in, b_in, w_mid, b_mid, w_out, b_out)
+    return (prices, *finish(big, small, squares))
 
 
 def solution(mesh):

time: 122 us -> 122 us (level)
  no operation moved by 1% of the time
where the time goes in v4:
time: 122 us
  Pallas kernels  119 us (98%)
  local copies, waits for them, and re-layouts  1.88 us (2%)
  between operations  1.31 us (1%)
    pallas_call x1, Pallas kernels, train(): pl.pallas_call(train_kernel, in_specs=[vmem] * 8 + [smem], out_specs=[vme...  67.8 us
    pallas_call x1, Pallas kernels, price_sums(): pl.pallas_call(prices_kernel, grid=(BLOCKS,), in_specs=[pl.BlockSpec((4,...  45.8 us
    pallas_call x1, Pallas kernels, finish(): pl.pallas_call(finish_kernel, grid=(TILES,), in_specs=[pl.BlockSpec((NC,...  5.1 us

profile of v4, /device:TPU:1, one launch (start us, length us, event | category | flops | bytes accessed | tf_op | source)
XLA Modules:
  0.0 121.9 jit_solution(8574452595929957592)
XLA Ops:
  1.3 1.3 %reshape.40.w_out_ref = bf16[1,1024]{1,0:T(2,128)(2,1)} reshape(bf16[1024]{0:T(1024)(128)(2,1)} %param.16) | data formatting | bytes 4096 | tf_op jit(solution)/shard_map/reshape | solution.py:697
  2.6 45.8 %prices.1 = (f32[8,128]{1,0:T(8,128)}, f32[8,128]{1,0:T(8,128)}) custom-call(f32[4,2048]{1,0:T(4,128)} %bitcast.9, f32[8,128]{1,0:T(8,128)} %constant.4.clone.lag_ref, bf16[2,64,128]{2,1,0:T(8,128)(2,1)} %inc_ref.1), custom_call_target="tpu_custom_call" | custom-call | tf_op jit(solution)/shard_map/prices/pallas_call | solution.py:257
  48.4 67.8 %train.1 = (f32[8,88]{1,0:T(8,128)}, f32[2,2,1024,256]{3,2,1,0:T(8,128)}, f32[2,16,512]{2,1,0:T(8,128)}, f32[2,8,256]{2,1,0:T(8,128)}) custom-call(f32[8,128]{1,0:T(8,128)} %get-tuple-element.19.sets_ref, f32[88,128]{1,0:T(8,128)} %constant.5.clone.table_ref, f32[8,128]{1,0:T(8,128)} %get-tuple-element.20.prices_ref, bf16[6,1024]{1,0:T(8,128)(2,1)} %w_in_ref.1, ...), custom_call_target="tpu_custom_call" | custom-call | tf_op jit(solution)/shard_map/train/pallas_call | solution.py:651
  116.2 0.0 copy-start
  116.2 5.1 %finish.1 = (f32[6,1024]{1,0:T(8,128)}, f32[1,1024]{1,0:T(1,128)}, f32[1024,1024]{1,0:T(8,128)}, f32[1,1024]{1,0:T(1,128)}, f32[1,1024]{1,0:T(1,128)}, /*index=5*/f32[1,1]{1,0:T(1,128)}) custom-call(f32[2,2,1024,256]{3,2,1,0:T(8,128)} %get-tuple-element.22.big_ref, f32[2,16,512]{2,1,0:T(8,128)} %get-tuple-element.23.small_ref, ...), custom_call_target="tpu_custom_call" | custom-call | tf_op jit(solution)/shard_map/finish/pallas_call | solution.py:742
  121.3 0.0 copy-done
  121.3 0.6 copy.19
Async XLA Ops:
  116.2 5.1 %copy-start = (f32[8,88]{1,0:T(8,128)S(1)}, f32[8,88]{1,0:T(8,128)}, u32[]{:S(2)}) copy-start(f32[8,88]{1,0:T(8,128)} %get-tuple-element.38) | copy-start | bytes 8452

commit v5 on v3

--- a/solution.py
+++ b/solution.py
@@ -284,7 +284,10 @@
             pltpu.SemaphoreType.DMA((NZ,)),
             pltpu.SemaphoreType.DMA((NZ,)),
         ],
-        compiler_params=pltpu.CompilerParams(collective_id=0, has_side_effects=True),
+        compiler_params=pltpu.CompilerParams(collective_id=0, has_side_effects=True, vmem_limit_bytes=24 * 1024 * 1024),
+        cost_estimate=pl.CostEstimate(
+            flops=20 * 1000 * 1000 * 1000, bytes_accessed=1000 * 1000, transcendentals=18 * 1000 * 1000
+        ),
         name="prices",
     )(params.T, jnp.asarray(lag_tables()), increments)
 
@@ -340,7 +343,7 @@
     scaled = (sets_ref[...] * factor)[None, :, :]
     prices = prices_ref[:, :PAIRS] / TOTAL_PATHS
     prices_out[...] = prices
-    w_out = w_out_ref[...].astype(f32)
+    w_out = w_out_ref[...].reshape(1, WIDE).astype(f32)
     g_out = jnp.zeros((8, WIDE), f32)
     g_bmid = jnp.zeros((8, WIDE), f32)
     g_bin = jnp.zeros((8, WIDE), f32)
@@ -620,7 +623,7 @@
             pltpu.SemaphoreType.DMA((SENDS,)),
             pltpu.SemaphoreType.DMA((SENDS,)),
         ],
-        compiler_params=pltpu.CompilerParams(collective_id=1, has_side_effects=True),
+        compiler_params=pltpu.CompilerParams(collective_id=1, has_side_effects=True, vmem_limit_bytes=36 * 1024 * 1024),
         name="train",
     )(
         sets,
@@ -630,14 +633,25 @@
         b_in.reshape(1, WIDE),
         w_mid,
         b_mid.reshape(1, WIDE),
-        w_out.reshape(1, WIDE),
+        w_out,
         b_out.reshape(1, 1),
     )
 
 
 def finish_kernel(
-    big_ref, small_ref, w_in_out, b_in_out, w_mid_out, b_mid_out, w_out_out, b_out_out
+    prices_ref,
+    big_ref,
+    small_ref,
+    prices_out,
+    w_in_out,
+    b_in_out,
+    w_mid_out,
+    b_mid_out,
+    w_out_out,
+    b_out_out,
 ):
+    prices_out[...] = prices_ref[...]
+
     def factor(total, entries):
         return lax.rsqrt(total * (1.0 / entries) + EPSILON)
 
@@ -662,24 +676,25 @@
         w_mid_out[:, pl.ds(c * HALF, HALF)] = big_ref[c] * f_mid
 
 
-def finish(big, small):
+def finish(prices, big, small):
     f32 = jnp.float32
     vmem = pl.BlockSpec(memory_space=pltpu.VMEM)
-    shapes = [(6, WIDE), (1, WIDE), (WIDE, WIDE), (1, WIDE), (1, WIDE), (1, 1)]
-    w_in, b_in, w_mid, b_mid, w_out, b_out = pl.pallas_call(
+    shapes = [(OWN, PAIRS), (6, WIDE), (1, WIDE), (WIDE, WIDE), (1, WIDE), (1, WIDE), (1, 1)]
+    prices, w_in, b_in, w_mid, b_mid, w_out, b_out = pl.pallas_call(
         finish_kernel,
-        in_specs=[vmem] * 2,
-        out_specs=[vmem] * 6,
+        in_specs=[vmem] * 3,
+        out_specs=[vmem] * 7,
         out_shape=[jax.ShapeDtypeStruct(shape, f32) for shape in shapes],
-        name="finish",
-    )(big, small)
-    return w_in, b_in.reshape(WIDE), w_mid, b_mid.reshape(WIDE), w_out.reshape(WIDE), b_out.reshape(1)
+        compiler_params=pltpu.CompilerParams(vmem_limit_bytes=16 * 1024 * 1024), name="finish",
+    )(prices, big, small)
+    b_in, b_mid, w_out = b_in.reshape(WIDE), b_mid.reshape(WIDE), w_out.reshape(WIDE)
+    return prices, w_in, b_in, w_mid, b_mid, w_out, b_out.reshape(1)
 
 
 def on_device(params, increments, w_in, b_in, w_mid, b_mid, w_out, b_out):
     sums, sets = price_sums(params, increments)
     prices, big, small = train(sets, sums, w_in, b_in, w_mid, b_mid, w_out, b_out)
-    return (prices, *finish(big, small))
+    return finish(prices, big, small)
 
 
 def solution(mesh):

time: 122 us -> 116 us (0.951)
  Pallas kernels: 118 us -> 112 us
    pallas_call x1, Pallas kernels: 67.5 us -> 64.5 us  [train(): pl.pallas_call(train_kernel, in_specs=[vmem] * 8 + [smem], out_specs=[vme...]
    pallas_call x1, Pallas kernels: 4.89 us -> 2.69 us  [finish(): pl.pallas_call(finish_kernel, in_specs=[vmem] * 3, out_specs=[vmem] * 7,...]
    unnamed x3 -> x18, local copies, waits for them, and re-layouts: 0.6 us -> 2.22 us
    reshape x1 -> x0, local copies, waits for them, and re-layouts: 1.28 us -> none  [train(): w_out.reshape(1, WIDE)]
where the time goes in v5:
time: 116 us
  Pallas kernels  112 us (97%)
  local copies, waits for them, and re-layouts  2.22 us (2%)
  between operations  1.38 us (1%)
    pallas_call x1, Pallas kernels, train(): pl.pallas_call(train_kernel, in_specs=[vmem] * 8 + [smem], out_specs=[vme...  64.5 us
    pallas_call x1, Pallas kernels, price_sums(): pl.pallas_call(prices_kernel, grid=(BLOCKS,), in_specs=[pl.BlockSpec((4,...  45 us
    pallas_call x1, Pallas kernels, finish(): pl.pallas_call(finish_kernel, in_specs=[vmem] * 3, out_specs=[vmem] * 7,...  2.69 us

profile of v5, /device:TPU:1, one launch (start us, length us, event | category | flops | bytes accessed | tf_op | source)
XLA Modules:
  0.0 115.7 jit_solution(14867950703841761801)
XLA Ops:
  1.3 0.0 copy-start.6
  1.3 0.7 copy-done.6
  2.0 0.0 copy-start.7
  2.0 0.8 copy-done.7
  2.8 0.0 copy-start.8
  2.8 0.7 copy-done.8
  3.5 0.0 copy-start
  3.5 0.0 copy-start.1
  3.5 0.0 copy-start.2
  3.5 0.0 copy-start.3
  3.5 0.0 copy-start.4
  3.5 0.0 copy-start.5
  3.5 45.0 %prices.1 = (f32[8,128]{1,0:T(8,128)S(1)}, f32[8,128]{1,0:T(8,128)S(1)}) custom-call(f32[4,2048]{1,0:T(4,128)S(1)} %bitcast.11, f32[8,128]{1,0:T(8,128)S(1)} %copy-done.8, bf16[2,64,128]{2,1,0:T(8,128)(2,1)S(1)} %copy-done.7), custom_call_target="tpu_custom_call" | custom-call | flops 20000000000 | bytes 1000000 | tf_op jit(solution)/shard_map/prices/pallas_call | solution.py:257
  48.5 0.0 copy-done
  48.5 0.0 copy-done.1
  48.5 0.0 copy-done.2
  48.5 0.0 copy-done.3
  48.6 0.0 copy-done.4
  48.6 0.0 copy-done.5
  48.6 64.5 %train.1 = (f32[8,88]{1,0:T(8,128)S(1)}, f32[2,1024,512]{2,1,0:T(8,128)S(1)}, f32[2,16,512]{2,1,0:T(8,128)S(1)}) custom-call(f32[8,128]{1,0:T(8,128)S(1)} %get-tuple-element.19.sets_ref, f32[88,128]{1,0:T(8,128)S(1)} %copy-done.1, f32[8,128]{1,0:T(8,128)S(1)} %get-tuple-element.20.prices_ref, bf16[6,1024]{1,0:T(8,128)(2,1)S(1)} %copy-done.2, ...), custom_call_target="tpu_custom_call" | custom-call | tf_op jit(solution)/shard_map/train/pallas_call | solution.py:593
  113.0 2.7 %finish.1 = (f32[8,88]{1,0:T(8,128)}, f32[6,1024]{1,0:T(8,128)}, f32[1,1024]{1,0:T(1,128)}, f32[1024,1024]{1,0:T(8,128)}, f32[1,1024]{1,0:T(1,128)}, /*index=5*/f32[1,1024]{1,0:T(1,128)}, f32[1,1]{1,0:T(1,128)}) custom-call(f32[8,88]{1,0:T(8,128)S(1)} %get-tuple-element.21.prices_ref, f32[2,1024,512]{2,1,0:T(8,128)S(1)} %get-tuple-element.22.big_ref, ...), custom_call_target="tpu_custom_call" | custom-call | tf_op jit(solution)/shard_map/finish/pallas_call | solution.py:683
Async XLA Ops:
  1.3 0.8 copy-start.6
  2.0 0.8 copy-start.7
  2.8 0.7 copy-start.8
  3.5 45.0 %copy-start = (bf16[1024,1024]{1,0:T(8,128)(2,1)S(1)}, bf16[1024,1024]{1,0:T(8,128)(2,1)}, u32[]{:S(2)}) copy-start(bf16[1024,1024]{1,0:T(8,128)(2,1)} %w_mid_ref.1) | copy-start | bytes 6291460
  3.5 45.0 %copy-start.1 = (f32[88,128]{1,0:T(8,128)S(1)}, f32[88,128]{1,0:T(8,128)}, u32[]{:S(2)}) copy-start(f32[88,128]{1,0:T(8,128)} %constant.5.clone.table_ref) | copy-start | bytes 135172
  3.5 45.0 %copy-start.2 = (bf16[6,1024]{1,0:T(8,128)(2,1)S(1)}, bf16[6,1024]{1,0:T(8,128)(2,1)}, u32[]{:S(2)}) copy-start(bf16[6,1024]{1,0:T(8,128)(2,1)} %w_in_ref.1) | copy-start | bytes 36868
  3.5 45.1 %copy-start.3 = (f32[1024]{0:T(1024)S(1)}, f32[1024]{0:T(1024)}, u32[]{:S(2)}) copy-start(f32[1024]{0:T(1024)} %param.13) | copy-start | bytes 12292
  3.5 45.1 %copy-start.4 = (f32[1024]{0:T(1024)S(1)}, f32[1024]{0:T(1024)}, u32[]{:S(2)}) copy-start(f32[1024]{0:T(1024)} %param.15) | copy-start | bytes 12292
  3.5 45.1 %copy-start.5 = (bf16[1024]{0:T(1024)(128)(2,1)S(1)}, bf16[1024]{0:T(1024)(128)(2,1)}, u32[]{:S(2)}) copy-start(bf16[1024]{0:T(1024)(128)(2,1)} %w_out_ref.1) | copy-start | bytes 6148

commit v6 on v5

v6 whole, which is shorter than its diff:
```python
import math

import jax
import jax.numpy as jnp
import numpy as np
from jax import lax
from jax.experimental import pallas as pl
from jax.experimental.pallas import tpu as pltpu
from jax.sharding import PartitionSpec as P

STEPS = 64
MATS = 8
STRIKES = 11
PAIRS = 88
EPSILON = 1e-06
LOG2E = 1.4426950408889634
NX, NY, NZ, NC = 4, 4, 8, 2
OWN = 8
BLOCK = NY * NZ * OWN
BLOCKS = NX * NC
SETS = 2048
TOTAL_PATHS = 32768
MESH = pl.DeviceIdType.MESH


def strike_values():
    return [
        [math.exp(0.05 * (j - 5) * math.sqrt((m + 1) / MATS)) for j in range(STRIKES)]
        for m in range(MATS)
    ]


def coords(index):
    core = index % NC
    z = (index // NC) % NZ
    y = (index // (NC * NZ)) % NY
    x = index // (NC * NZ * NY)
    return x, y, z, core


def device_at(x, y, z, core):
    return ((x * NY + y) * NZ + z) * NC + core


def lag_tables():
    lag = np.tile(np.arange(STEPS, dtype=np.float64), 2)
    table = np.zeros((8, 128), np.float32)
    table[0] = np.log2(np.maximum(lag, 1.0))
    table[1] = np.log2(np.maximum(lag - 1.0, 1.0))
    table[2] = np.log2(np.maximum(lag, 1.0) / STEPS)
    return table


def set_operands(sets, lag_ref, rows, ratio, scale):
    f32, bf16 = jnp.float32, jnp.bfloat16
    shape = (sets.shape[0], 128)
    hurst, vol, correl, forward = (
        jnp.broadcast_to(sets[:, k : k + 1], shape) for k in range(4)
    )
    lane = lax.broadcasted_iota(jnp.int32, shape, 1)
    upper = lane >= STEPS
    lag = jnp.where(upper, lane - STEPS, lane)
    expo = hurst + 0.5
    late = jnp.where(lag >= 2, jnp.exp2(expo * lag_ref[1:2, :]), 0.0)
    powers = jnp.exp2(expo * lag_ref[0:1, :]) - late
    front = jnp.sqrt(2.0 * hurst) * jnp.exp2(-6.0 * hurst) / expo
    kern = jnp.where(lag >= 1, powers * front, 0.0).astype(bf16).astype(f32)
    half = (0.5 * LOG2E) * vol
    weight = kern * half
    comp = (-0.5 * vol * half) * jnp.exp2((2.0 * hurst) * lag_ref[2:3, :])
    rest = 1.0 - correl * correl
    const = (0.5 * LOG2E) * jnp.log(forward * (1.0 / STEPS) / rest) - 1.0
    w_hi = weight.astype(bf16).astype(f32)
    c_hi = comp.astype(bf16).astype(f32)
    k_hi = const.astype(bf16).astype(f32)
    k_rest = const - k_hi
    k_lo = k_rest.astype(bf16).astype(f32)
    first = lag == 0
    kern_row = jnp.where(first, jnp.where(upper, k_lo, k_hi), jnp.where(upper, weight - w_hi, w_hi))
    comp_row = jnp.where(
        first, jnp.where(upper, 0.0, k_rest - k_lo), jnp.where(upper, comp - c_hi, c_hi)
    )
    rows[:, 0:128] = kern_row.astype(bf16)
    rows[:, 128:256] = comp_row.astype(bf16)
    ratio[...] = correl * lax.rsqrt(rest)
    scale[...] = (2.0 * LOG2E) * rest


def price_peers(x, y, z, core):
    mine = x * NC + core
    blocks = []
    for b in range(BLOCKS - 1):
        other = (mine + 1 + b) % BLOCKS
        blocks.append(device_at(other // NC, y, z, other % NC))
    along_y = [device_at(x, (y + d) % NY, z, core) for d in range(1, NY)]
    along_z = [device_at(x, y, (z + d) % NZ, core) for d in range(1, NZ)]
    return blocks, along_y, along_z


def prices_part(
    params_ref,
    lag_ref,
    inc_ref,
    between,
    sets,
    rows_ref,
    ratio_ref,
    scale_ref,
    noise,
    table,
    walk,
    part,
    sent,
    got,
    got_y,
    got_z,
    send_sem,
    got_sem,
    send_y,
    got_y_sem,
    send_z,
    got_z_sem,
):
    x, y, z, core = coords(lax.axis_index("paths"))
    blocks, along_y, along_z = price_peers(x, y, z, core)
    for k in range(NX * NY):
        some = params_ref[:, pl.ds(k * 128, 128)]
        some = jnp.concatenate([some, jnp.zeros((124, 128), jnp.float32)], axis=0).T
        sets[k // NY, pl.ds((k % NY) * NZ, NZ)] = some.reshape(NZ, NC, OWN, 128)
    noise[0] = inc_ref[0].astype(jnp.float32)
    noise[1] = inc_ref[1].astype(jnp.float32)
    part[...] = jnp.zeros_like(part)
    row = lax.broadcasted_iota(jnp.int32, (STEPS, 128), 0)
    for j in range(STEPS):
        walk[pl.ds(STEPS - 1 - j, 1), :] = noise[0, pl.ds(j, 1), :]
    walk[pl.ds(STEPS, STEPS), :] = jnp.zeros((STEPS, 128), jnp.float32)
    one = jnp.ones((STEPS, 128), jnp.float32)
    for i in range(STEPS):
        past = walk[pl.ds(STEPS - 1 - i, STEPS), :]
        past = jnp.where(row == 0, one, past).astype(jnp.bfloat16)
        pick = jnp.where(row == i, 1.0, 0.0)
        hot = jnp.where(row == 0, one, pick).astype(jnp.bfloat16)
        hot_lo = jnp.where(row == 0, 0.0, pick).astype(jnp.bfloat16)
        cols = pl.ds((i % 2) * 128, 128)
        table[i // 2, pl.ds(0, STEPS), cols] = past
        table[i // 2, pl.ds(STEPS, STEPS), cols] = past
        table[i // 2, pl.ds(2 * STEPS, STEPS), cols] = hot
        table[i // 2, pl.ds(3 * STEPS, STEPS), cols] = hot_lo

    def block_copy(b):
        other = (x * NC + core + 1 + b) % BLOCKS
        return pltpu.make_async_remote_copy(
            src_ref=sent.at[b],
            dst_ref=got.at[b],
            send_sem=send_sem.at[b],
            recv_sem=got_sem.at[b],
            device_id=(device_at(other // NC, y, z, other % NC),),
            device_id_type=MESH,
        )

    def one_block(step, carry):
        strikes = strike_values()
        other = (x * NC + core + 1 + step) % BLOCKS
        block = sets[other // NC, :, other % NC].reshape(BLOCK, 128)
        set_operands(block, lag_ref, rows_ref, ratio_ref, scale_ref)
        walk[...] = jnp.zeros_like(walk)
        for m in range(MATS):
            for q in range(4):
                pair = jnp.dot(
                    rows_ref[...], table[m * 4 + q], preferred_element_type=jnp.float32
                )
                for h in range(2):
                    i = m * 8 + q * 2 + h
                    vol = jnp.exp2(pair[:, h * 128 : (h + 1) * 128])
                    shock = ratio_ref[...] * noise[0, pl.ds(i, 1), :] + noise[1, pl.ds(i, 1), :]
                    walk[...] += vol * (shock - vol)
            spot = jnp.exp2((walk[...] * scale_ref[...]).T)
            for j in range(STRIKES):
                k = strikes[m][j]
                top = jnp.sum(jnp.maximum(spot, k).reshape(16, 8, BLOCK), axis=0)
                part[pl.ds(m * STRIKES + j, 1), :] = jnp.sum(top - 16.0 * k, axis=0, keepdims=True)
        sent[step] = part[...].T

        @pl.when(step == 0)
        def _():
            pl.semaphore_wait(pltpu.get_barrier_semaphore(), len(blocks + along_y + along_z))

        @pl.when(step < BLOCKS - 1)
        def _():
            block_copy(step).start()

        return carry

    lax.fori_loop(0, BLOCKS, one_block, 0)
    total = sent.at[BLOCKS - 1]
    for b in range(BLOCKS - 1):
        block_copy(b).wait_recv()
        total[...] += got[b]
    rows_y = NZ * OWN

    def y_rows(d):
        return pl.ds(pl.multiple_of(((y + d) % NY) * rows_y, rows_y), rows_y)

    copies = []
    for d in range(1, NY):
        copy = pltpu.make_async_remote_copy(
            src_ref=total.at[y_rows(d), :],
            dst_ref=got_y.at[d],
            send_sem=send_y.at[d],
            recv_sem=got_y_sem.at[d],
            device_id=(along_y[d - 1],),
            device_id_type=MESH,
        )
        copy.start()
        copies.append(copy)
    own = total[y_rows(0), :]
    for d in range(1, NY):
        copies[d - 1].wait_recv()
        own = own + got_y[d]
    got_y[0] = own

    def z_rows(d):
        return pl.ds(pl.multiple_of(((z + d) % NZ) * OWN, OWN), OWN)

    for d in range(1, NZ):
        copy = pltpu.make_async_remote_copy(
            src_ref=got_y.at[0, z_rows(d), :],
            dst_ref=got_z.at[d],
            send_sem=send_z.at[d],
            recv_sem=got_z_sem.at[d],
            device_id=(along_z[d - 1],),
            device_id_type=MESH,
        )
        copy.start()
        copies.append(copy)
    between(sets.at[x, y * NZ + z, core])
    final = got_y[0, z_rows(0), :]
    for d in range(1, NZ):
        copies[NY - 1 + d - 1].wait_recv()
        final = final + got_z[d]
    for b in range(BLOCKS - 1):
        block_copy(b).wait_send()
    for copy in copies:
        copy.wait_send()
    return final


WIDE = 1024
HALF = WIDE // NC
ROWS_A = WIDE // NX
ROWS_B = ROWS_A // NY
ROWS_Z = ROWS_B // NZ
SMALL = 16
SLICE = HALF // NX


ROWS = PAIRS * OWN
CHUNK = ROWS // 4
DEPTH = 768


def pair_table():
    tenors = (np.arange(MATS, dtype=np.float32) + np.float32(1.0)) / np.float32(MATS)
    offsets = np.arange(STRIKES, dtype=np.float32) - np.float32((STRIKES - 1) / 2.0)
    log_strike = np.float32(0.05) * offsets[None, :] * np.sqrt(tenors)[:, None]
    table = np.zeros((PAIRS, 128), np.float32)
    table[:, 4] = np.float32(4.0) * log_strike.reshape(PAIRS)
    table[:, 5] = np.repeat(tenors, STRIKES)
    table[:, 6] = 1.0
    return table


def forward_part(
    sets_ref, table_ref, w_in_ref, b_in_ref, w_mid_ref, b_mid_ref, w_out_ref, b_out_ref,
    feats, hid_in, slope_in, hid_mid, slope_mid, pred,
):
    f32, bf16 = jnp.float32, jnp.bfloat16
    pairs = CHUNK // OWN
    lane = lax.broadcasted_iota(jnp.int32, (OWN, 128), 1)
    factor = jnp.where(lane == 0, 4.0, jnp.where(lane == 3, 20.0, 1.0))
    scaled = (sets_ref[...] * factor)[None, :, :]
    w_out = w_out_ref[...].reshape(1, WIDE).astype(f32)
    for c in range(ROWS // CHUNK):
        rows = pl.ds(c * CHUNK, CHUNK)
        table = table_ref[pl.ds(c * pairs, pairs), :]
        x = (table[:, None, :] + scaled).reshape(CHUNK, 128).astype(bf16)
        feats[rows, :] = x
        raw = jnp.dot(x[:, :6], w_in_ref[...], preferred_element_type=f32) + b_in_ref[...]
        g = jax.nn.sigmoid(raw)
        hid = (raw * g).astype(bf16)
        hid_in[rows, :] = hid
        slope_in[rows, :] = g * (1.0 + raw * (1.0 - g))
        raw = jnp.dot(hid, w_mid_ref[...], preferred_element_type=f32) + b_mid_ref[...]
        g = jax.nn.sigmoid(raw)
        mid = (raw * g).astype(bf16)
        hid_mid[rows, :] = mid
        slope_mid[rows, :] = g * (1.0 + raw * (1.0 - g))
        pred[rows, :] = jnp.sum(mid.astype(f32) * w_out, axis=1, keepdims=True) + b_out_ref[0, 0]
    hid_in[pl.ds(ROWS, DEPTH - ROWS), :] = jnp.zeros((DEPTH - ROWS, WIDE), bf16)


def backward_part(
    prices, w_mid_ref, w_out_ref, small_ref,
    feats, hid_in, slope_in, hid_mid, slope_mid, pred, delta_mid, delta_in, hid_turn,
):
    f32, bf16 = jnp.float32, jnp.bfloat16
    pairs = CHUNK // OWN
    w_out = w_out_ref[...].reshape(1, WIDE).astype(f32)
    g_out = jnp.zeros((8, WIDE), f32)
    g_bmid = jnp.zeros((8, WIDE), f32)
    g_bin = jnp.zeros((8, WIDE), f32)
    g_bout = jnp.zeros((8, 1), f32)
    delta_mid[pl.ds(ROWS, DEPTH - ROWS), :] = jnp.zeros((DEPTH - ROWS, WIDE), bf16)
    for c in range(ROWS // CHUNK):
        rows = pl.ds(c * CHUNK, CHUNK)
        target = jnp.concatenate(
            [prices[:, k : k + 1] for k in range(c * pairs, (c + 1) * pairs)], axis=0
        )
        slope = (pred[rows, :] - target) * (1.0 / SETS)
        mid = hid_mid[rows, :].astype(f32)
        g_bout = g_bout + jnp.sum(slope.reshape(pairs, 8, 1), axis=0)
        g_out = g_out + jnp.sum((mid * slope).reshape(pairs, 8, WIDE), axis=0)
        delta = (slope * w_out * slope_mid[rows, :]).astype(bf16)
        delta_mid[rows, :] = delta
        g_bmid = g_bmid + jnp.sum(delta.astype(f32).reshape(pairs, 8, WIDE), axis=0)
        back = lax.dot_general(
            delta, w_mid_ref[...], (((1,), (1,)), ((), ())), preferred_element_type=f32
        )
        inner = (back * slope_in[rows, :]).astype(bf16)
        delta_in[rows, :] = inner
        g_bin = g_bin + jnp.sum(inner.astype(f32).reshape(pairs, 8, WIDE), axis=0)
    small_ref[pl.ds(0, 8), :] = lax.dot_general(
        feats[:, :8], delta_in[...], (((0,), (0,)), ((), ())), preferred_element_type=f32
    )
    small_ref[pl.ds(6, 1), :] = jnp.sum(g_bin, axis=0, keepdims=True)
    small_ref[pl.ds(7, 1), :] = jnp.sum(g_bmid, axis=0, keepdims=True)
    small_ref[pl.ds(8, 1), :] = jnp.sum(g_out, axis=0, keepdims=True)
    small_ref[pl.ds(9, 1), :] = jnp.broadcast_to(jnp.sum(g_bout, axis=0, keepdims=True), (1, WIDE))
    small_ref[pl.ds(10, 6), :] = jnp.zeros((6, WIDE), f32)


LATER = (2, 1, 3, 0)
SENDS = 100


def step_kernel(
    params_hbm,
    lag_hbm,
    inc_hbm,
    w_mid_hbm,
    table_hbm,
    w_in_hbm,
    b_in_hbm,
    b_mid_hbm,
    w_out_hbm,
    b_out_ref,
    prices_out,
    big_out,
    small_out,
    params_ref,
    lag_ref,
    inc_ref,
    w_mid_ref,
    table_ref,
    w_in_ref,
    b_in_ref,
    b_mid_ref,
    w_out_ref,
    load_sem,
    p_sets,
    p_rows_ref,
    p_ratio_ref,
    p_scale_ref,
    p_noise,
    p_table,
    p_walk,
    p_part,
    p_sent,
    p_got,
    p_got_y,
    p_got_z,
    p_send_sem,
    p_got_sem,
    p_send_y,
    p_got_y_sem,
    p_send_z,
    p_got_z_sem,
    small,
    feats,
    hid_in,
    slope_in,
    hid_mid,
    slope_mid,
    pred,
    delta_mid,
    delta_in,
    hid_turn,
    other,
    got_c,
    work,
    got_a,
    far_a,
    far_b,
    mid,
    got_b,
    low,
    got_z,
    s_got_c,
    s_got_a,
    s_b,
    s_z,
    s_sum,
    t_send_sem,
    t_recv_sem,
):
    x, y, z, core = coords(lax.axis_index("paths"))
    a = x * (1 - core) + y * core
    b = y * (1 - core) + x * core

    def at(aa, bb, zz):
        return device_at(aa * (1 - core) + bb * core, bb * (1 - core) + aa * core, zz, core)

    partner = device_at(x, y, z, 1 - core)
    along_a = [at((a + d) % NX, b, z) for d in range(1, NX)]
    along_b = [at(a, (b + d) % NY, z) for d in range(1, NY)]
    along_z = [at(a, b, (z + d) % NZ) for d in range(1, NZ)]
    barrier = pltpu.get_barrier_semaphore()
    for group in price_peers(x, y, z, core):
        for peer in group:
            pl.semaphore_signal(barrier, inc=1, device_id=(peer,), device_id_type=MESH)
    loads = []
    for k, (far, near) in enumerate(
        (
            (params_hbm, params_ref),
            (lag_hbm, lag_ref),
            (inc_hbm, inc_ref),
            (w_mid_hbm, w_mid_ref),
            (table_hbm, table_ref),
            (w_in_hbm, w_in_ref),
            (b_in_hbm, b_in_ref),
            (b_mid_hbm, b_mid_ref),
            (w_out_hbm, w_out_ref),
        )
    ):
        copy = pltpu.make_async_copy(far, near, load_sem.at[k])
        copy.start()
        loads.append(copy)
    for copy in loads[:3]:
        copy.wait()

    def forward(own):
        for copy in loads[3:]:
            copy.wait()
        forward_part(
            own, table_ref, w_in_ref, b_in_ref, w_mid_ref, b_mid_ref, w_out_ref, b_out_ref,
            feats, hid_in, slope_in, hid_mid, slope_mid, pred,
        )

    sums = prices_part(
        params_ref,
        lag_ref,
        inc_ref,
        forward,
        p_sets,
        p_rows_ref,
        p_ratio_ref,
        p_scale_ref,
        p_noise,
        p_table,
        p_walk,
        p_part,
        p_sent,
        p_got,
        p_got_y,
        p_got_z,
        p_send_sem,
        p_got_sem,
        p_send_y,
        p_got_y_sem,
        p_send_z,
        p_got_z_sem,
    )
    prices = sums[:, :PAIRS] / TOTAL_PATHS
    prices_out[...] = prices
    backward_part(
        prices, w_mid_ref, w_out_ref, small,
        feats, hid_in, slope_in, hid_mid, slope_mid, pred, delta_mid, delta_in, hid_turn,
    )
    hid_turn[...] = hid_in[...].T

    count = [0]
    started = []

    def send(src, dst, peer):
        k = count[0]
        count[0] += 1
        copy = pltpu.make_async_remote_copy(
            src_ref=src,
            dst_ref=dst,
            send_sem=t_send_sem.at[k],
            recv_sem=t_recv_sem.at[k],
            device_id=(peer,),
            device_id_type=MESH,
        )
        copy.start()
        started.append(copy)
        return copy

    def part(index, size):
        return pl.ds(pl.multiple_of(index * size, size), size)

    def rows_of(aa, bb):
        return part((aa % NX) * NY + bb % NY, ROWS_B)

    def product(first, second, e, cols):
        left = jnp.concatenate(
            [hid_turn[rows_of(first + d, second + e), :] for d in range(NX)], axis=0
        )
        out = jnp.dot(left, delta_mid[:, cols], preferred_element_type=jnp.float32)
        return out.reshape(NX, ROWS_B, HALF)

    own_cols, other_cols = part(core, HALF), part(1 - core, HALF)
    little = send(small.at[:, other_cols], s_got_c, partner)
    pair = {}
    for e in LATER:
        other[e] = product(b, a, e, other_cols)
        pair[e] = send(other.at[e], got_c.at[e], partner)
    little.wait_recv()
    s_got_c[...] += small[:, own_cols]
    littles = []
    for d in range(1, NX):
        littles.append(
            send(s_got_c.at[:, part((a + d) % NX, SLICE)], s_got_a.at[d - 1], along_a[d - 1])
        )
    near_a, near_b = [along_a[0], along_a[2]], [along_b[0], along_b[2]]
    top, bottom = pl.ds(0, ROWS_B // 2), pl.ds(ROWS_B // 2, ROWS_B // 2)
    steps, ahead = {}, {}
    for e in LATER:
        mine = product(a, b, e, own_cols)
        pair[e].wait_recv()
        work[e] = mine + got_c[e]
        ahead[e] = [
            send(work.at[e, 2, top], far_a.at[e, 0], near_a[0]),
            send(work.at[e, 2, bottom], far_a.at[e, 1], near_a[1]),
        ]
    for e in LATER:
        ahead[e][0].wait_recv()
        work[e, 1, top] += far_a[e, 0]
        steps[e] = [send(work.at[e, 1], got_a.at[e, 0], near_a[0])]
        ahead[e][1].wait_recv()
        work[e, 3, bottom] += far_a[e, 1]
        steps[e].append(send(work.at[e, 3], got_a.at[e, 1], near_a[1]))
    for copy in littles:
        copy.wait_recv()
    s_b[b] = s_got_c[:, part(a, SLICE)] + s_got_a[0] + s_got_a[1] + s_got_a[2]
    littles = [send(s_b.at[b], s_b.at[b], peer) for peer in along_b]
    for e in LATER:
        for copy in steps[e]:
            copy.wait_recv()
        mid[e] = work[e, 0] + got_a[e, 0] + got_a[e, 1]
        if e == 2:
            beyond = [
                send(mid.at[2, top], far_b.at[0], near_b[0]),
                send(mid.at[2, bottom], far_b.at[1], near_b[1]),
            ]
    beyond[0].wait_recv()
    mid[1, top] += far_b[0]
    across = [send(mid.at[1], got_b.at[0], near_b[0])]
    beyond[1].wait_recv()
    mid[3, bottom] += far_b[1]
    across.append(send(mid.at[3], got_b.at[1], near_b[1]))
    for copy in littles:
        copy.wait_recv()
    s_z[z] = (s_b[0] + s_b[1]) + (s_b[2] + s_b[3])
    littles = [send(s_z.at[z], s_z.at[z], peer) for peer in along_z]
    for copy in across:
        copy.wait_recv()
    low[...] = mid[0] + got_b[0] + got_b[1]
    deep = [
        send(low.at[part((z + d) % NZ, ROWS_Z), :], got_z.at[d - 1], along_z[d - 1])
        for d in range(1, NZ)
    ]
    for copy in littles:
        copy.wait_recv()
    s_all = ((s_z[0] + s_z[1]) + (s_z[2] + s_z[3])) + ((s_z[4] + s_z[5]) + (s_z[6] + s_z[7]))
    s_sum[:, part(a, SLICE)] = s_all
    littles = [
        send(s_sum.at[:, part(a, SLICE)], s_sum.at[:, part(a, SLICE)], peer) for peer in along_a
    ]
    final = low[part(z, ROWS_Z), :]
    for d in range(1, NZ):
        deep[d - 1].wait_recv()
        final = final + got_z[d - 1]

    half_out = big_out.at[core]
    mine = part((a * NY + b) * NZ + z, ROWS_Z)
    half_out[mine, :] = final
    deep = [send(half_out.at[mine, :], half_out.at[mine, :], peer) for peer in along_z]
    for copy in littles:
        copy.wait_recv()
    small_out[core] = s_sum[...]
    little = send(small_out.at[core], small_out.at[core], partner)
    for copy in deep:
        copy.wait_recv()

    def spread(rows, targets):
        return [send(half_out.at[rows, :], half_out.at[rows, :], peer) for peer in targets]

    def top_of(aa, bb):
        return part(((aa % NX) * NY + bb % NY) * 2, ROWS_B // 2)

    def bottom_of(aa, bb):
        return part(((aa % NX) * NY + bb % NY) * 2 + 1, ROWS_B // 2)

    near_a, near_b = [along_a[0], along_a[2]], [along_b[0], along_b[2]]
    across = spread(rows_of(a, b), near_b)
    steps = [spread(rows_of(a, b), near_a)]
    pairs = spread(rows_of(a, b), [partner])
    relays_b, relays_a = [], {}

    def pass_on(e, bb):
        steps[e][0].wait_recv()
        first = spread(top_of(a + 3, bb), near_a[:1])
        pairs.extend(spread(rows_of(a + 3, bb), [partner]))
        steps[e][1].wait_recv()
        second = spread(bottom_of(a + 1, bb), near_a[1:])
        pairs.extend(spread(rows_of(a + 1, bb), [partner]))
        relays_a[e] = first + second

    across[0].wait_recv()
    relays_b += spread(top_of(a, b + 3), near_b[:1])
    steps.append(spread(rows_of(a, b + 3), near_a))
    across[1].wait_recv()
    relays_b += spread(bottom_of(a, b + 1), near_b[1:])
    steps.append(spread(rows_of(a, b + 1), near_a))
    pairs += spread(rows_of(a, b + 3), [partner]) + spread(rows_of(a, b + 1), [partner])
    pass_on(0, b)
    for copy in relays_b:
        copy.wait_recv()
    steps.append(spread(rows_of(a, b + 2), near_a))
    pairs += spread(rows_of(a, b + 2), [partner])
    pass_on(1, b + 3)
    pass_on(2, b + 1)
    pass_on(3, b + 2)
    for e, bb in enumerate((b, b + 3, b + 1, b + 2)):
        for copy in relays_a[e]:
            copy.wait_recv()
        pairs += spread(rows_of(a + 2, bb), [partner])
    little.wait_recv()
    for copy in pairs:
        copy.wait_recv()
    for copy in started:
        copy.wait_send()


def train(params, increments, w_in, b_in, w_mid, b_mid, w_out, b_out):
    f32, bf16 = jnp.float32, jnp.bfloat16
    vmem = pl.BlockSpec(memory_space=pltpu.VMEM)
    smem = pl.BlockSpec(memory_space=pltpu.SMEM)
    hbm = pl.BlockSpec(memory_space=pltpu.HBM)
    loads = [
        params.T,
        jnp.asarray(lag_tables()),
        increments,
        w_mid,
        jnp.asarray(pair_table()),
        w_in,
        b_in.reshape(1, WIDE),
        b_mid.reshape(1, WIDE),
        w_out,
    ]
    return pl.pallas_call(
        step_kernel,
        in_specs=[hbm] * 9 + [smem],
        out_specs=[vmem, vmem, vmem],
        out_shape=[
            jax.ShapeDtypeStruct((OWN, PAIRS), f32),
            jax.ShapeDtypeStruct((NC, WIDE, HALF), f32),
            jax.ShapeDtypeStruct((NC, SMALL, HALF), f32),
        ],
        scratch_shapes=[
            pltpu.VMEM((4, SETS), f32),
            pltpu.VMEM((8, 128), f32),
            pltpu.VMEM((2, STEPS, 128), bf16),
            pltpu.VMEM((WIDE, WIDE), bf16),
            pltpu.VMEM((PAIRS, 128), f32),
            pltpu.VMEM((6, WIDE), bf16),
            pltpu.VMEM((1, WIDE), f32),
            pltpu.VMEM((1, WIDE), f32),
            pltpu.VMEM((WIDE,), bf16),
            pltpu.SemaphoreType.DMA((9,)),
            pltpu.VMEM((NX, NY * NZ, NC, OWN, 128), f32),
            pltpu.VMEM((BLOCK, 256), bf16),
            pltpu.VMEM((BLOCK, 128), f32),
            pltpu.VMEM((BLOCK, 128), f32),
            pltpu.VMEM((2, STEPS, 128), f32),
            pltpu.VMEM((STEPS // 2, 256, 256), bf16),
            pltpu.VMEM((BLOCK, 128), f32),
            pltpu.VMEM((128, BLOCK), f32),
            pltpu.VMEM((BLOCKS, BLOCK, 128), f32),
            pltpu.VMEM((BLOCKS - 1, BLOCK, 128), f32),
            pltpu.VMEM((NY, NZ * OWN, 128), f32),
            pltpu.VMEM((NZ, OWN, 128), f32),
            pltpu.SemaphoreType.DMA((BLOCKS,)),
            pltpu.SemaphoreType.DMA((BLOCKS,)),
            pltpu.SemaphoreType.DMA((NY,)),
            pltpu.SemaphoreType.DMA((NY,)),
            pltpu.SemaphoreType.DMA((NZ,)),
            pltpu.SemaphoreType.DMA((NZ,)),
            pltpu.VMEM((SMALL, WIDE), f32),
            pltpu.VMEM((ROWS, 128), bf16),
            pltpu.VMEM((DEPTH, WIDE), bf16),
            pltpu.VMEM((ROWS, WIDE), f32),
            pltpu.VMEM((ROWS, WIDE), bf16),
            pltpu.VMEM((ROWS, WIDE), f32),
            pltpu.VMEM((ROWS, 1), f32),
            pltpu.VMEM((DEPTH, WIDE), bf16),
            pltpu.VMEM((ROWS, WIDE), bf16),
            pltpu.VMEM((WIDE, DEPTH), bf16),
            pltpu.VMEM((NY, NX, ROWS_B, HALF), f32),
            pltpu.VMEM((NY, NX, ROWS_B, HALF), f32),
            pltpu.VMEM((NY, NX, ROWS_B, HALF), f32),
            pltpu.VMEM((NY, 2, ROWS_B, HALF), f32),
            pltpu.VMEM((NY, 2, ROWS_B // 2, HALF), f32),
            pltpu.VMEM((2, ROWS_B // 2, HALF), f32),
            pltpu.VMEM((NY, ROWS_B, HALF), f32),
            pltpu.VMEM((2, ROWS_B, HALF), f32),
            pltpu.VMEM((ROWS_B, HALF), f32),
            pltpu.VMEM((NZ - 1, ROWS_Z, HALF), f32),
            pltpu.VMEM((SMALL, HALF), f32),
            pltpu.VMEM((NX - 1, SMALL, SLICE), f32),
            pltpu.VMEM((NY, SMALL, SLICE), f32),
            pltpu.VMEM((NZ, SMALL, SLICE), f32),
            pltpu.VMEM((SMALL, HALF), f32),
            pltpu.SemaphoreType.DMA((SENDS,)),
            pltpu.SemaphoreType.DMA((SENDS,)),
        ],
        compiler_params=pltpu.CompilerParams(
            collective_id=0, has_side_effects=True, vmem_limit_bytes=46 * 1024 * 1024
        ),
        name="step",
    )(
        *[pltpu.with_memory_space_constraint(value, pltpu.HBM) for value in loads],
        b_out.reshape(1, 1),
    )


def finish_kernel(
    prices_ref,
    big_ref,
    small_ref,
    prices_out,
    w_in_out,
    b_in_out,
    w_mid_out,
    b_mid_out,
    w_out_out,
    b_out_out,
):
    prices_out[...] = prices_ref[...]

    def factor(total, entries):
        return lax.rsqrt(total * (1.0 / entries) + EPSILON)

    def sumsq(value):
        return jnp.sum(jnp.sum(value * value, axis=1, keepdims=True), axis=0, keepdims=True)

    small = jnp.concatenate([small_ref[0], small_ref[1]], axis=1)
    g_bout = small[9:10, 0:1]
    s_mid = sumsq(small[7:8])
    for k in range(8):
        for c in range(NC):
            s_mid = s_mid + sumsq(big_ref[c, pl.ds(k * 128, 128), :])
    f_in = factor(sumsq(small[0:7]), 7 * WIDE)
    f_mid = factor(s_mid, (WIDE + 1) * WIDE)
    f_out = factor(sumsq(small[8:9]) + g_bout * g_bout, WIDE + 1)
    w_in_out[...] = small[0:6] * f_in
    b_in_out[...] = small[6:7] * f_in
    b_mid_out[...] = small[7:8] * f_mid
    w_out_out[...] = small[8:9] * f_out
    b_out_out[...] = g_bout * f_out
    for c in range(NC):
        w_mid_out[:, pl.ds(c * HALF, HALF)] = big_ref[c] * f_mid


def finish(prices, big, small):
    f32 = jnp.float32
    vmem = pl.BlockSpec(memory_space=pltpu.VMEM)
    shapes = [(OWN, PAIRS), (6, WIDE), (1, WIDE), (WIDE, WIDE), (1, WIDE), (1, WIDE), (1, 1)]
    prices, w_in, b_in, w_mid, b_mid, w_out, b_out = pl.pallas_call(
        finish_kernel,
        in_specs=[vmem] * 3,
        out_specs=[vmem] * 7,
        out_shape=[jax.ShapeDtypeStruct(shape, f32) for shape in shapes],
        compiler_params=pltpu.CompilerParams(vmem_limit_bytes=16 * 1024 * 1024), name="finish",
    )(prices, big, small)
    b_in, b_mid, w_out = b_in.reshape(WIDE), b_mid.reshape(WIDE), w_out.reshape(WIDE)
    return prices, w_in, b_in, w_mid, b_mid, w_out, b_out.reshape(1)


def on_device(params, increments, w_in, b_in, w_mid, b_mid, w_out, b_out):
    prices, big, small = train(params, increments, w_in, b_in, w_mid, b_mid, w_out, b_out)
    return finish(prices, big, small)


def solution(mesh):
    in_specs = (P(), P(None, None, "paths"), P(), P(), P(), P(), P(), P())
    out_specs = (P("paths", None), P(), P(), P(), P(), P(), P())
    return jax.shard_map(
        on_device, mesh=mesh, in_specs=in_specs, out_specs=out_specs, check_vma=False
    )
```

time: 116 us -> 106 us (0.914)
  Pallas kernels: 112 us -> 105 us
  local copies, waits for them, and re-layouts: 2.22 us -> 0 us
    pallas_call x2 -> x1, Pallas kernels: 109 us -> 102 us  [train(): pl.pallas_call(step_kernel, in_specs=[hbm] * 9 + [smem], out_specs=[vmem,...]
    unnamed x18 -> x0, local copies, waits for them, and re-layouts: 2.22 us -> none
where the time goes in v6:
time: 106 us
  Pallas kernels  105 us (99%)
  between operations  1.29 us (1%)
    pallas_call x1, Pallas kernels, train(): pl.pallas_call(step_kernel, in_specs=[hbm] * 9 + [smem], out_specs=[vmem,...  102 us
    pallas_call x1, Pallas kernels, finish(): pl.pallas_call(finish_kernel, in_specs=[vmem] * 3, out_specs=[vmem] * 7,...  2.69 us

profile of v6, /device:TPU:1, one launch (start us, length us, event | category | flops | bytes accessed | tf_op | source)
XLA Modules:
  0.0 105.9 jit_solution(7054385105212518781)
XLA Ops:
  1.3 101.9 %step.1 = (f32[8,88]{1,0:T(8,128)S(1)}, f32[2,1024,512]{2,1,0:T(8,128)S(1)}, f32[2,16,512]{2,1,0:T(8,128)S(1)}) custom-call(f32[4,2048]{1,0:T(4,128)} %bitcast.9, f32[8,128]{1,0:T(8,128)} %constant.4.clone.lag_hbm, bf16[2,64,128]{2,1,0:T(8,128)(2,1)} %inc_hbm.1, bf16[1024,1024]{1,0:T(8,128)(2,1)} %w_mid_hbm.1, f32[88,128]{1,0:T(8,128)} %constant.5.clone.table_hbm, ...), custom_call_target="tpu_custom_call" | custom-call | tf_op jit(solution)/shard_map/step/pallas_call | solution.py:672
  103.2 2.7 %finish.1 = (f32[8,88]{1,0:T(8,128)}, f32[6,1024]{1,0:T(8,128)}, f32[1,1024]{1,0:T(1,128)}, f32[1024,1024]{1,0:T(8,128)}, f32[1,1024]{1,0:T(1,128)}, /*index=5*/f32[1,1024]{1,0:T(1,128)}, f32[1,1]{1,0:T(1,128)}) custom-call(f32[8,88]{1,0:T(8,128)S(1)} %get-tuple-element.17.prices_ref, f32[2,1024,512]{2,1,0:T(8,128)S(1)} %get-tuple-element.18.big_ref, ...), custom_call_target="tpu_custom_call" | custom-call | tf_op jit(solution)/shard_map/finish/pallas_call | solution.py:790

commit v7 on v6

--- a/solution.py
+++ b/solution.py
@@ -255,7 +255,7 @@
 
 
 ROWS = PAIRS * OWN
-CHUNK = ROWS // 4
+CHUNK = ROWS // 2
 DEPTH = 768
 
 
@@ -272,7 +272,7 @@
 
 def forward_part(
     sets_ref, table_ref, w_in_ref, b_in_ref, w_mid_ref, b_mid_ref, w_out_ref, b_out_ref,
-    feats, hid_in, slope_in, hid_mid, slope_mid, pred,
+    feats, hid_in, slope_in, hid_mid, slope_mid, pred, hid_turn,
 ):
     f32, bf16 = jnp.float32, jnp.bfloat16
     pairs = CHUNK // OWN
@@ -297,11 +297,12 @@
         slope_mid[rows, :] = g * (1.0 + raw * (1.0 - g))
         pred[rows, :] = jnp.sum(mid.astype(f32) * w_out, axis=1, keepdims=True) + b_out_ref[0, 0]
     hid_in[pl.ds(ROWS, DEPTH - ROWS), :] = jnp.zeros((DEPTH - ROWS, WIDE), bf16)
+    hid_turn[...] = hid_in[...].T
 
 
 def backward_part(
     prices, w_mid_ref, w_out_ref, small_ref,
-    feats, hid_in, slope_in, hid_mid, slope_mid, pred, delta_mid, delta_in, hid_turn,
+    feats, hid_in, slope_in, hid_mid, slope_mid, pred, delta_mid, delta_in,
 ):
     f32, bf16 = jnp.float32, jnp.bfloat16
     pairs = CHUNK // OWN
@@ -453,7 +454,7 @@
             copy.wait()
         forward_part(
             own, table_ref, w_in_ref, b_in_ref, w_mid_ref, b_mid_ref, w_out_ref, b_out_ref,
-            feats, hid_in, slope_in, hid_mid, slope_mid, pred,
+            feats, hid_in, slope_in, hid_mid, slope_mid, pred, hid_turn,
         )
 
     sums = prices_part(
@@ -484,9 +485,8 @@
     prices_out[...] = prices
     backward_part(
         prices, w_mid_ref, w_out_ref, small,
-        feats, hid_in, slope_in, hid_mid, slope_mid, pred, delta_mid, delta_in, hid_turn,
+        feats, hid_in, slope_in, hid_mid, slope_mid, pred, delta_mid, delta_in,
     )
-    hid_turn[...] = hid_in[...].T
 
     count = [0]
     started = []
@@ -554,21 +554,25 @@
         copy.wait_recv()
     s_b[b] = s_got_c[:, part(a, SLICE)] + s_got_a[0] + s_got_a[1] + s_got_a[2]
     littles = [send(s_b.at[b], s_b.at[b], peer) for peer in along_b]
-    for e in LATER:
+    def collect(e):
         for copy in steps[e]:
             copy.wait_recv()
         mid[e] = work[e, 0] + got_a[e, 0] + got_a[e, 1]
-        if e == 2:
-            beyond = [
-                send(mid.at[2, top], far_b.at[0], near_b[0]),
-                send(mid.at[2, bottom], far_b.at[1], near_b[1]),
-            ]
+
+    collect(2)
+    beyond = [
+        send(mid.at[2, top], far_b.at[0], near_b[0]),
+        send(mid.at[2, bottom], far_b.at[1], near_b[1]),
+    ]
+    collect(1)
     beyond[0].wait_recv()
     mid[1, top] += far_b[0]
     across = [send(mid.at[1], got_b.at[0], near_b[0])]
+    collect(3)
     beyond[1].wait_recv()
     mid[3, bottom] += far_b[1]
     across.append(send(mid.at[3], got_b.at[1], near_b[1]))
+    collect(0)
     for copy in littles:
         copy.wait_recv()
     s_z[z] = (s_b[0] + s_b[1]) + (s_b[2] + s_b[3])

time: 106 us -> 104 us (0.981)
  Pallas kernels: 105 us -> 102 us
    pallas_call x1, Pallas kernels: 102 us -> 99.8 us  [train(): pl.pallas_call(step_kernel, in_specs=[hbm] * 9 + [smem], out_specs=[vmem,...]
where the time goes in v7:
time: 104 us
  Pallas kernels  102 us (98%)
  between operations  1.29 us (1%)
    pallas_call x1, Pallas kernels, train(): pl.pallas_call(step_kernel, in_specs=[hbm] * 9 + [smem], out_specs=[vmem,...  99.8 us
    pallas_call x1, Pallas kernels, finish(): pl.pallas_call(finish_kernel, in_specs=[vmem] * 3, out_specs=[vmem] * 7,...  2.69 us

profile of v7, /device:TPU:1, one launch (start us, length us, event | category | flops | bytes accessed | tf_op | source)
XLA Modules:
  0.0 103.8 jit_solution(6915378378482932192)
XLA Ops:
  1.3 99.8 %step.1 = (f32[8,88]{1,0:T(8,128)S(1)}, f32[2,1024,512]{2,1,0:T(8,128)S(1)}, f32[2,16,512]{2,1,0:T(8,128)S(1)}) custom-call(f32[4,2048]{1,0:T(4,128)} %bitcast.9, f32[8,128]{1,0:T(8,128)} %constant.4.clone.lag_hbm, bf16[2,64,128]{2,1,0:T(8,128)(2,1)} %inc_hbm.1, bf16[1024,1024]{1,0:T(8,128)(2,1)} %w_mid_hbm.1, f32[88,128]{1,0:T(8,128)} %constant.5.clone.table_hbm, ...), custom_call_target="tpu_custom_call" | custom-call | tf_op jit(solution)/shard_map/step/pallas_call | solution.py:676
  101.1 2.7 %finish.1 = (f32[8,88]{1,0:T(8,128)}, f32[6,1024]{1,0:T(8,128)}, f32[1,1024]{1,0:T(1,128)}, f32[1024,1024]{1,0:T(8,128)}, f32[1,1024]{1,0:T(1,128)}, /*index=5*/f32[1,1024]{1,0:T(1,128)}, f32[1,1]{1,0:T(1,128)}) custom-call(f32[8,88]{1,0:T(8,128)S(1)} %get-tuple-element.17.prices_ref, f32[2,1024,512]{2,1,0:T(8,128)S(1)} %get-tuple-element.18.big_ref, ...), custom_call_target="tpu_custom_call" | custom-call | tf_op jit(solution)/shard_map/finish/pallas_call | solution.py:794
